TPU v7x, 32 devices: a whole 2x2x4 slice. The times are simulated.
32 devices in a mesh: tok: 16 (over z, y, core), head: 2 (over x).
Axes of the slice: x: 2, y: 2, z: 4, core: 2. Of those that a mesh axis runs over, the one named last changes fastest.
Arguments:
- hidden: bfloat16 [8192, 5120], P('tok', 'head'), may hold values from -6 to 6
- w_latent: bfloat16 [5120, 512], P('head'), may hold values from -0.078125 to 0.078125
- w_rope: bfloat16 [5120, 64], P('head'), may hold values from -0.078125 to 0.078125
- kv_gain: float32 [512], replicated, may hold values from 0.25 to 1.75
- q_latent: bfloat16 [16, 32, 64, 512], P('tok', None, 'head'), may hold values from -105 to 105
- q_rope: bfloat16 [16, 32, 4096], P('tok', None, 'head'), may hold values from -6 to 6
- w_value: bfloat16 [64, 512, 128], P('head'), may hold values from -0.25 to 0.25
- page_table: int32 [16, 10], replicated, may hold values from -1 to 63, as said below
- dest_group: int32 [16], replicated, may hold values from 0 to 15, each once
- ctx_len: int32 [16], replicated, may hold values from 1 to 1280, as said below
Outputs:
- attn_out: bfloat16 [16, 32, 8192], P('tok', 'head')
Inputs may be any that keep to these rules, and one draw needn't show every extreme that they name: `page_table`: row r lists request r's pages in context order, then -1; every page appears in exactly one row; no row holds two pages p whose p // 4 is equal; some row holds 10 pages. Request r's listed pages number ctx_len[r] / 128 rounded up. `dest_group`: every group serves exactly one request.
All inputs are finite; a program needn't handle non-finite values.
Results may differ from a plain program's by a relative error of at most 0.012.
The roundings to bfloat16 on the way count: a program that leaves them out, or rounds other values in their place, can miss the bound.
Values may be sent and summed in bfloat16 or wider, within the bound.
No kernel may reach another device: no remote copies, remote signals or barrier semaphores. Data moves between devices by JAX's collectives and lax.ppermute only.
A program may use at most 64 MiB of HBM per device.

v0:
```python
import functools

import jax
import jax.numpy as jnp
import numpy as np
from jax import lax
from jax.experimental import pallas as pl
from jax.experimental.pallas import tpu as pltpu
from jax.sharding import PartitionSpec as P


PAGE = 128
LANES = 128
EPS = 1e-06
SCALE = 192.0 ** (-0.5)
THETA = 10000.0
LOG2E = 1.4426950408889634
FLOOR = -1e30
BF16, F32 = jnp.bfloat16, jnp.float32


MIB = 1024 * 1024


def params(mib):
    return pltpu.CompilerParams(vmem_limit_bytes=mib * MIB)


def nt_dot(a, b):
    return lax.dot_general(a, b, (((1,), (1,)), ((), ())), preferred_element_type=F32)


def project_kernel(
    share_ref, hid_ref, wl_ref, wr_ref, *refs, chunks, pages, tokens, parts, shares
):
    outs, (hid_buf, wl_buf, wr_buf, sems) = refs[:chunks], refs[chunks:]
    share = tokens * chunks
    half = tokens // 2
    depth = hid_ref.shape[-1] // parts
    copies = []
    for k in range(parts):
        at = pl.ds(k * depth, depth)
        copies.append(
            [
                pltpu.make_async_copy(wl_ref.at[at], wl_buf.at[at], sems.at[0, k]),
                pltpu.make_async_copy(wr_ref.at[:, at], wr_buf.at[:, at], sems.at[1, k]),
            ]
            + [
                pltpu.make_async_copy(
                    hid_ref.at[:, share_ref[s], :, at], hid_buf.at[s, :, :, at], sems.at[2 + s, k]
                )
                for s in range(shares)
            ]
        )
    for group in copies:
        for copy in group:
            copy.start()
    for s in range(shares):
        lat = rope = None
        for k in range(parts):
            for copy in copies[k] if s == 0 else ():
                copy.wait()
            rows = hid_buf[s, :, :, k * depth : (k + 1) * depth].reshape(pages * share, depth)
            wide = jnp.dot(rows, wl_buf[k * depth : (k + 1) * depth], preferred_element_type=F32)
            side = nt_dot(rows, wr_buf[:, k * depth : (k + 1) * depth])
            lat, rope = (wide, side) if k == 0 else (lat + wide, rope + side)
        blocks = lat.shape[1] // LANES
        for page in range(pages):
            for c in range(chunks):
                at = (page * chunks + c) * tokens
                for b in range(blocks):
                    outs[c][s, page, b * tokens : (b + 1) * tokens] = lat[
                        at : at + tokens, b * LANES : (b + 1) * LANES
                    ]
                outs[c][s, page, blocks * tokens :] = jnp.concatenate(
                    [rope[at : at + half], rope[at + half : at + tokens]], axis=1
                )


def project(hidden, w_latent, w_rope, shares, head_count, chunks):
    features = hidden.shape[1]
    pages = hidden.shape[0] // PAGE
    share = PAGE // head_count
    tokens = share // chunks
    parts = next(n for n in (5, 4, 2, 1) if features % (n * LANES) == 0)
    rows = tokens * (w_latent.shape[1] // LANES) + tokens // 2
    count = shares.shape[0]
    view = hidden.reshape(pages, head_count, share, features)
    side = w_rope.T
    hbm = pl.BlockSpec(memory_space=pltpu.HBM)
    flops = 2 * count * pages * share * features * (w_latent.shape[1] + w_rope.shape[1])
    return pl.pallas_call(
        functools.partial(
            project_kernel, chunks=chunks, pages=pages, tokens=tokens, parts=parts, shares=count
        ),
        in_specs=[pl.BlockSpec(memory_space=pltpu.SMEM), hbm, hbm, hbm],
        out_specs=[pl.BlockSpec(memory_space=pltpu.VMEM)] * chunks,
        out_shape=[jax.ShapeDtypeStruct((count, pages, rows, LANES), F32)] * chunks,
        scratch_shapes=[
            pltpu.VMEM((count, pages, share, features), BF16),
            pltpu.VMEM(w_latent.shape, BF16),
            pltpu.VMEM(side.shape, BF16),
            pltpu.SemaphoreType.DMA((2 + count, parts)),
        ],
        compiler_params=params(63),
        cost_estimate=pl.CostEstimate(
            flops=flops,
            bytes_accessed=2 * features * (count * pages * share + w_latent.shape[1] + LANES),
            transcendentals=0,
        ),
    )(shares, view, w_latent, side)


def request_of(dest_ref, group):
    def look(i, found):
        return jnp.where(dest_ref[i] == group, i, found)

    return lax.fori_loop(0, dest_ref.shape[0], look, 0)


def finish_kernel(dest_ref, table_ref, gain_ref, freq_ref, own_ref, *refs, tokens, blocks, chunk, share):
    terms, outs, page_ref = refs[:-3], refs[-3:-1], refs[-1]
    me, head = lax.axis_index("tok"), lax.axis_index("head")
    pages = own_ref.shape[1]
    half = tokens // 2
    table = table_ref[...]
    request = lax.broadcasted_iota(jnp.int32, table.shape, 0)
    listed = lax.broadcasted_iota(jnp.int32, table.shape, 1)
    lane = lax.broadcasted_iota(jnp.int32, (half, LANES), 1)
    row = lax.broadcasted_iota(jnp.int32, (half, LANES), 0)
    low = (lane % 64) < 32
    inside = row + (lane // 64) * half + (head * share + chunk * tokens)
    for page in range(pages):
        hit = table == me * pages + page
        slot = jnp.sum(jnp.where(hit, listed, 0))
        group = dest_ref[jnp.sum(jnp.where(hit, request, 0))]

        def total(lo, hi, page=page):
            value = own_ref[0, page, lo:hi]
            for term in terms:
                value = value + term[page, lo:hi]
            return value

        parts = [total(b * tokens, (b + 1) * tokens) for b in range(blocks)]
        square = parts[0] * parts[0]
        for part in parts[1:]:
            square = square + part * part
        mean = jnp.sum(square, axis=1, keepdims=True) * (1.0 / (blocks * LANES))
        inverse = lax.rsqrt(mean + EPS)
        scaled = [(part * inverse * gain_ref[b : b + 1]).astype(BF16) for b, part in enumerate(parts)]
        raw = total(blocks * tokens, blocks * tokens + half).astype(BF16).astype(F32)
        other = jnp.where(low, -pltpu.roll(raw, LANES - 32, 1), pltpu.roll(raw, 32, 1))
        angle = freq_ref[...] * (inside + slot * PAGE).astype(F32)
        turned = raw * jnp.cos(angle) + other * jnp.sin(angle)
        page_ref[page, : blocks * tokens] = jnp.concatenate(scaled, axis=0)
        page_ref[page, blocks * tokens :] = turned.astype(BF16)
        place = lax.bitwise_xor(group // 2, me // 2)
        same = group % 2 == me % 2

        @pl.when(same)
        def _(page=page, place=place):
            outs[0][place] = page_ref[page]

        @pl.when(jnp.logical_not(same))
        def _(page=page, place=place):
            outs[1][place] = page_ref[page]


def finish(dest, table, gain, freq, own, terms, tokens, chunk, share):
    _, pages, rows, _ = own.shape
    blocks = gain.shape[0]
    vmem = pl.BlockSpec(memory_space=pltpu.VMEM)
    half_groups = max(dest.shape[0] // 2, 1)
    return pl.pallas_call(
        functools.partial(finish_kernel, tokens=tokens, blocks=blocks, chunk=chunk, share=share),
        in_specs=[pl.BlockSpec(memory_space=pltpu.SMEM)] + [vmem] * (4 + len(terms)),
        out_specs=[vmem] * 2,
        out_shape=[jax.ShapeDtypeStruct((half_groups, rows, LANES), BF16)] * 2,
        scratch_shapes=[pltpu.VMEM((pages, rows, LANES), BF16)],
        compiler_params=params(8),
    )(dest, table, gain, freq, own, *terms)


def select_kernel(dest_ref, table_ref, in_ref, out_ref, *, pages):
    me = lax.axis_index("tok")
    request = request_of(dest_ref, me)
    first = table_ref[request, 0]
    for slot in range(out_ref.shape[0]):
        listed = table_ref[request, slot]
        source = lax.div(jnp.where(listed >= 0, listed, first), pages)
        place = lax.bitwise_xor(lax.div(source, 2), lax.div(me, 2))
        out_ref[slot] = in_ref[place, lax.rem(source + me, 2)]


def select(dest, table, arrived, pages):
    vmem, smem = pl.BlockSpec(memory_space=pltpu.VMEM), pl.BlockSpec(memory_space=pltpu.SMEM)
    return pl.pallas_call(
        functools.partial(select_kernel, pages=pages),
        in_specs=[smem, smem, vmem],
        out_specs=vmem,
        out_shape=jax.ShapeDtypeStruct((table.shape[1],) + arrived.shape[2:], BF16),
        compiler_params=params(8),
    )(dest, table, arrived)


def fold(value, op):
    width = value.shape[1]
    while width > LANES and width % (2 * LANES) == 0:
        width //= 2
        value = op(value[:, :width], value[:, width:])
    return value


def attend_kernel(
    dest_ref, len_ref, q_ref, w_ref, *refs, planes, chunks, tokens, blocks, rows_q, step
):
    payloads = refs[: planes * chunks]
    outs = refs[planes * chunks : planes * (chunks + 1)]
    key_ref, score_ref, acc_ref, top_ref, sum_ref, map_ref, w_buf, w_sem = refs[planes * (chunks + 1) :]
    w_copy = pltpu.make_async_copy(w_ref, w_buf, w_sem)
    w_copy.start()
    head = lax.axis_index("head")
    context = len_ref[request_of(dest_ref, lax.axis_index("tok"))]
    share = tokens * chunks
    width = blocks * LANES
    count = q_ref.shape[0]
    steps = lax.div(context + (step - 1), step)
    live = steps * (step // PAGE)

    for plane in range(planes):
        for chunk in range(chunks):
            payload = payloads[plane * chunks + chunk]
            offset = lax.rem(head + (planes - plane), planes) * share + chunk * tokens

            def fill(slot, _, payload=payload, offset=offset):
                at = pl.multiple_of(slot * PAGE + offset, tokens)
                for b in range(blocks):
                    key_ref[pl.ds(at, tokens), b * LANES : (b + 1) * LANES] = payload[
                        slot, b * tokens : (b + 1) * tokens
                    ]
                packed = payload[slot, width * tokens // LANES :].astype(F32)
                swapped = pltpu.roll(packed, 64, 1)
                key_ref[pl.ds(at, tokens), width:] = jnp.concatenate([packed, swapped], axis=0).astype(BF16)
                return 0

            lax.fori_loop(0, live, fill, 0)

    top_ref[...] = jnp.full_like(top_ref, FLOOR)

    def score_step(i, _):
        at = pl.multiple_of(i * step, step)
        scores = nt_dot(q_ref[...], key_ref[pl.ds(at, step)])
        position = at + lax.broadcasted_iota(jnp.int32, (1, step), 1)
        scores = scores + jnp.where(position < context, 0.0, FLOOR)
        score_ref[i] = scores
        top_ref[...] = jnp.maximum(top_ref[...], fold(scores, jnp.maximum))
        return 0

    lax.fori_loop(0, steps, score_step, 0)
    top = jnp.max(top_ref[...], axis=1, keepdims=True)
    acc_ref[...] = jnp.zeros_like(acc_ref)
    sum_ref[...] = jnp.zeros_like(sum_ref)

    def value_step(i, _):
        at = pl.multiple_of(i * step, step)
        weights = jnp.exp2((score_ref[i] - top) * (SCALE * LOG2E))
        acc_ref[...] += jnp.dot(
            weights.astype(BF16), key_ref[pl.ds(at, step), :width], preferred_element_type=F32
        )
        sum_ref[...] += fold(weights, jnp.add)
        return 0

    lax.fori_loop(0, steps, value_step, 0)
    owned = rows_q // planes
    inverse = 1.0 / jnp.sum(sum_ref[...], axis=1, keepdims=True)
    w_copy.wait()
    for h in range(count // rows_q):
        rows = slice(h * rows_q, (h + 1) * rows_q)
        attended = (acc_ref[rows] * inverse[rows]).astype(BF16)
        mapped = jnp.dot(attended, w_buf[h], preferred_element_type=F32)
        for p in range(planes):
            map_ref[p, :, h * LANES : (h + 1) * LANES] = mapped[p * owned : (p + 1) * owned]
    for d in range(planes):
        outs[d][...] = map_ref[lax.rem(head + d, planes)].astype(BF16)


def attend(dest, ctx_len, query, w_value, payloads, planes, chunks, tokens):
    heads, lat, _ = w_value.shape
    count = query.shape[0]
    rows_q = count // heads
    slots = payloads[0].shape[0]
    step = 2 * PAGE if slots % 2 == 0 else PAGE
    keys = slots * PAGE
    vmem, smem = pl.BlockSpec(memory_space=pltpu.VMEM), pl.BlockSpec(memory_space=pltpu.SMEM)
    return pl.pallas_call(
        functools.partial(
            attend_kernel,
            planes=planes,
            chunks=chunks,
            tokens=tokens,
            blocks=lat // LANES,
            rows_q=rows_q,
            step=step,
        ),
        in_specs=[smem, smem, vmem, pl.BlockSpec(memory_space=pltpu.HBM)] + [vmem] * len(payloads),
        out_specs=[vmem] * planes,
        out_shape=[jax.ShapeDtypeStruct((rows_q // planes, heads * LANES), BF16)] * planes,
        scratch_shapes=[
            pltpu.VMEM((keys, lat + LANES), BF16),
            pltpu.VMEM((keys // step, count, step), F32),
            pltpu.VMEM((count, lat), F32),
            pltpu.VMEM((count, LANES), F32),
            pltpu.VMEM((count, LANES), F32),
            pltpu.VMEM((planes, rows_q // planes, heads * LANES), F32),
            pltpu.VMEM(w_value.shape, BF16),
            pltpu.SemaphoreType.DMA,
        ],
        compiler_params=params(60),
    )(dest, ctx_len, query, w_value, *payloads)


def shift(value, axis, by):
    count = lax.axis_size(axis)
    return lax.ppermute(value, axis, [(i, (i + by) % count) for i in range(count)])


def trade(value, mask):
    count = lax.axis_size("tok")
    return lax.ppermute(value, "tok", [(i, i ^ mask) for i in range(count)])


CHUNKS = 2


def run_device(
    hidden, w_latent, w_rope, kv_gain, q_latent, q_rope, w_value, page_table, dest_group, ctx_len
):
    groups, planes = lax.axis_size("tok"), lax.axis_size("head")
    my_head = lax.axis_index("head")
    pages = hidden.shape[0] // PAGE
    share = PAGE // planes
    chunks = CHUNKS if share // CHUNKS >= 16 else 1
    tokens = share // chunks
    blocks = w_latent.shape[1] // LANES
    rope_width = w_rope.shape[1]

    others = (my_head + 1 + jnp.arange(planes - 1, dtype=jnp.int32)) % planes
    sent = project(hidden, w_latent, w_rope, others.astype(jnp.int32), planes, chunks)
    arrived = []
    for c in range(chunks):
        arrived.append([shift(sent[c][d - 1], "head", d) for d in range(1, planes)])
    own = project(hidden, w_latent, w_rope, my_head[None].astype(jnp.int32), planes, chunks)

    rows_q, heads = q_latent.shape[1], q_latent.shape[2]
    query_side = q_rope[0].reshape(rows_q, heads, rope_width)
    query_side = jnp.pad(query_side, ((0, 0), (0, 0), (0, LANES - rope_width)))
    query = jnp.concatenate([q_latent[0], query_side], axis=2).transpose(1, 0, 2)
    query = query.reshape(heads * rows_q, -1)

    half_width = rope_width // 2
    freq = np.power(THETA, -2.0 * np.arange(half_width) / rope_width)
    freq = jnp.asarray(np.tile(freq, LANES // half_width)[None].astype(np.float32))
    gain = kv_gain.reshape(blocks, LANES)

    picked = []
    for c in range(chunks):
        mine, other = finish(
            dest_group, page_table, gain, freq, own[c], arrived[c], tokens, c, share
        )
        got = trade(other, 1)
        landed = [jnp.stack([mine[0], got[0]])]
        for k in range(1, groups // 2):
            landed.append(trade(jnp.stack([mine[k], got[k]]), 2 * k))
        picked.append(select(dest_group, page_table, jnp.stack(landed), pages))
    payloads = list(picked)
    for d in range(1, planes):
        for c in range(chunks):
            payloads.append(shift(picked[c], "head", d))
    mapped = attend(dest_group, ctx_len, query, w_value, payloads, planes, chunks, tokens)

    pieces = [mapped[0]] + [shift(mapped[d], "head", d) for d in range(1, planes)]
    columns = []
    for source in range(planes):
        behind = (my_head - source) % planes
        column = pieces[0]
        for d in range(1, planes):
            column = jnp.where(behind == d, pieces[d], column)
        columns.append(column)
    return jnp.concatenate(columns, axis=1)[None]


def solution(mesh):
    placed = (
        P("tok", "head"),
        P("head", None),
        P("head", None),
        P(),
        P("tok", None, "head", None),
        P("tok", None, "head"),
        P("head", None, None),
        P(),
        P(),
        P(),
    )
    return jax.shard_map(
        run_device, mesh=mesh, in_specs=placed, out_specs=P("tok", "head", None), check_vma=False
    )
```

profile of v0, /device:TPU:20, one launch (start us, length us, event | category | flops | bytes accessed | tf_op | source)
XLA Modules:
  0.0 92.0 jit_solution(2934068580968633206)
XLA Ops:
  0.0 4.0 %shard_map.110 = (f32[1,4,144,128]{3,2,1,0:T(8,128)}, f32[1,4,144,128]{3,2,1,0:T(8,128)}) custom-call(s32[1]{0:T(128)S(6)} %select_n.33.share_ref, bf16[4,2,64,2560]{3,2,1,0:T(8,128)(2,1)} %bitcast.51, bf16[2560,512]{1,0:T(8,128)(2,1)} %wl_ref.3, bf16[64,2560]{1,0:T(8,128)(2,1)} %bitcast.54), custom_call_target="tpu_custom_call" | custom-call | flops 754974720 | bytes 4587520 | tf_op jit(solution)/shard_map/pallas_call | solution.py:92
  4.0 1.6 %collective-permute-start = (f32[4,144,128]{2,1,0:T(8,128)}, f32[4,144,128]{2,1,0:T(8,128)S(1)}, u32[]{:S(2)}, u32[]{:S(2)}) collective-permute-start(f32[4,144,128]{2,1,0:T(8,128)} %bitcast.58), channel_id=1, source_target_pairs={{0,1},{1,0},{2,3},{3,2},{4,5},{5,4},{6,7},{7,6},{8,9},{9,8},{10,11... | collective-permute-start | bytes 884744 | tf_op jit(solution)/shard_map/ppermute | solution.py:324
  5.6 0.5 collective-permute-start.9
  6.1 4.0 %shard_map.109 = (f32[1,4,144,128]{3,2,1,0:T(8,128)}, f32[1,4,144,128]{3,2,1,0:T(8,128)}) custom-call(s32[1]{0:T(128)} %bitcast.4.share_ref, bf16[4,2,64,2560]{3,2,1,0:T(8,128)(2,1)} %bitcast.52, bf16[2560,512]{1,0:T(8,128)(2,1)} %wl_ref.3, bf16[64,2560]{1,0:T(8,128)(2,1)} %bitcast.55), custom_call_target="tpu_custom_call" | custom-call | flops 754974720 | bytes 4587520 | tf_op jit(solution)/shard_map/pallas_call | solution.py:92
  10.2 4.0 %collective-permute-done.refs_0_ = f32[4,144,128]{2,1,0:T(8,128)S(1)} collective-permute-done((f32[4,144,128]{2,1,0:T(8,128)}, f32[4,144,128]{2,1,0:T(8,128)S(1)}, u32[]{:S(2)}, u32[]{:S(2)}) %collective-permute-start) | collective-permute-done | bytes 294944 | tf_op jit(solution)/shard_map/ppermute | solution.py:324
  14.2 1.0 %copy-done.3 = f32[1,4,144,128]{3,2,1,0:T(8,128)S(1)} copy-done((f32[1,4,144,128]{3,2,1,0:T(8,128)S(1)}, f32[1,4,144,128]{3,2,1,0:T(8,128)}, u32[]{:S(2)}) %copy-start.3) | copy-done | bytes 294936
  15.2 1.3 %shard_map.111 = (bf16[8,144,128]{2,1,0:T(8,128)(2,1)S(1)}, bf16[8,144,128]{2,1,0:T(8,128)(2,1)S(1)}) custom-call(s32[16]{0:T(128)S(1)} %copy-done.5, s32[16,10]{1,0:T(8,128)S(1)} %copy-done.4, f32[4,128]{1,0:T(4,128)S(1)} %bitcast.49, f32[1,128]{1,0:T(1,128)S(1)} %copy-done.7, f32[1,4,144,128]{3,2,1,0:T(8,128)S(1)} %copy-done.3, ...), custom_call_target="tpu_custom_call" | custom-call | tf_op jit(solution)/shard_map/pallas_call | solution.py:174
  16.4 0.1 collective-permute-start.1
  16.6 2.8 %collective-permute-done.9.refs_0_ = f32[4,144,128]{2,1,0:T(8,128)S(1)} collective-permute-done((f32[4,144,128]{2,1,0:T(8,128)}, f32[4,144,128]{2,1,0:T(8,128)S(1)}, u32[]{:S(2)}, u32[]{:S(2)}) %collective-permute-start.9) | collective-permute-done | bytes 294944 | tf_op jit(solution)/shard_map/ppermute | solution.py:324
  19.4 1.0 %copy-done.2 = f32[1,4,144,128]{3,2,1,0:T(8,128)S(1)} copy-done((f32[1,4,144,128]{3,2,1,0:T(8,128)S(1)}, f32[1,4,144,128]{3,2,1,0:T(8,128)}, u32[]{:S(2)}) %copy-start.2) | copy-done | bytes 294936
  20.3 1.3 %shard_map.113 = (bf16[8,144,128]{2,1,0:T(8,128)(2,1)S(1)}, bf16[8,144,128]{2,1,0:T(8,128)(2,1)S(1)}) custom-call(s32[16]{0:T(128)S(1)} %copy-done.5, s32[16,10]{1,0:T(8,128)S(1)} %copy-done.4, f32[4,128]{1,0:T(4,128)S(1)} %bitcast.50, f32[1,128]{1,0:T(1,128)S(1)} %copy-done.7, f32[1,4,144,128]{3,2,1,0:T(8,128)S(1)} %copy-done.2, ...), custom_call_target="tpu_custom_call" | custom-call | tf_op jit(solution)/shard_map/pallas_call | solution.py:174
  21.6 0.1 collective-permute-start.10
  21.8 0.6 collective-permute-start.2
  22.4 1.6 %collective-permute-start.3 = (bf16[2,144,128]{2,1,0:T(8,128)(2,1)S(1)}, bf16[2,144,128]{2,1,0:T(8,128)(2,1)S(1)}, u32[]{:S(2)}, u32[]{:S(2)}) collective-permute-start(bf16[2,144,128]{2,1,0:T(8,128)(2,1)S(1)} %pad_maximum_fusion.1), channel_id=1, source_target_pairs={{0,8},{2,10},{4,12},{6,14},{8,0},{10,2},{12,4},{14,6},{16,24},{18,... | collective-permute-start | bytes 221192 | tf_op jit(solution)/shard_map/ppermute | solution.py:329
  24.0 1.5 %collective-permute-start.4 = (bf16[2,144,128]{2,1,0:T(8,128)(2,1)S(1)}, bf16[2,144,128]{2,1,0:T(8,128)(2,1)S(1)}, u32[]{:S(2)}, u32[]{:S(2)}) collective-permute-start(bf16[2,144,128]{2,1,0:T(8,128)(2,1)S(1)} %pad_maximum_fusion.2), channel_id=1, source_target_pairs={{0,12},{2,14},{4,8},{6,10},{8,4},{10,6},{12,0},{14,2},{16,28},{18,... | collective-permute-start | bytes 221192 | tf_op jit(solution)/shard_map/ppermute | solution.py:329
  25.5 0.4 collective-permute-start.5
  26.0 0.0 collective-permute-done.10
  26.0 2.6 %collective-permute-start.6 = (bf16[2,144,128]{2,1,0:T(8,128)(2,1)S(1)}, bf16[2,144,128]{2,1,0:T(8,128)(2,1)S(1)}, u32[]{:S(2)}, u32[]{:S(2)}) collective-permute-start(bf16[2,144,128]{2,1,0:T(8,128)(2,1)S(1)} %pad_maximum_fusion.4), channel_id=1, source_target_pairs={{0,20},{2,22},{4,16},{6,18},{8,28},{10,30},{12,24},{14,26},{16,4},... | collective-permute-start | bytes 221192 | tf_op jit(solution)/shard_map/ppermute | solution.py:329
  28.6 0.0 copy-start.11
  28.6 0.0 copy-start.8
  28.8 0.5 collective-permute-start.7
  29.3 2.6 %collective-permute-start.8 = (bf16[2,144,128]{2,1,0:T(8,128)(2,1)S(1)}, bf16[2,144,128]{2,1,0:T(8,128)(2,1)S(1)}, u32[]{:S(2)}, u32[]{:S(2)}) collective-permute-start(bf16[2,144,128]{2,1,0:T(8,128)(2,1)S(1)} %pad_maximum_fusion.6), channel_id=1, source_target_pairs={{0,28},{2,30},{4,24},{6,26},{8,20},{10,22},{12,16},{14,18},{16,12}... | collective-permute-start | bytes 221192 | tf_op jit(solution)/shard_map/ppermute | solution.py:329
  31.9 0.6 collective-permute-start.11
  32.5 5.6 %collective-permute-start.12 = (bf16[2,144,128]{2,1,0:T(8,128)(2,1)S(1)}, bf16[2,144,128]{2,1,0:T(8,128)(2,1)S(1)}, u32[]{:S(2)}, u32[]{:S(2)}) collective-permute-start(bf16[2,144,128]{2,1,0:T(8,128)(2,1)S(1)} %pad_maximum_fusion.8), channel_id=1, source_target_pairs={{0,8},{2,10},{4,12},{6,14},{8,0},{10,2},{12,4},{14,6},{16,24},{18,... | collective-permute-start | bytes 221192 | tf_op jit(solution)/shard_map/ppermute | solution.py:329
  38.2 2.5 %collective-permute-start.13 = (bf16[2,144,128]{2,1,0:T(8,128)(2,1)S(1)}, bf16[2,144,128]{2,1,0:T(8,128)(2,1)S(1)}, u32[]{:S(2)}, u32[]{:S(2)}) collective-permute-start(bf16[2,144,128]{2,1,0:T(8,128)(2,1)S(1)} %pad_maximum_fusion.9), channel_id=1, source_target_pairs={{0,12},{2,14},{4,8},{6,10},{8,4},{10,6},{12,0},{14,2},{16,28},{18,... | collective-permute-start | bytes 221192 | tf_op jit(solution)/shard_map/ppermute | solution.py:329
  40.7 0.1 collective-permute-start.14
  40.8 0.6 collective-permute-done.8
  41.3 2.9 %collective-permute-start.15 = (bf16[2,144,128]{2,1,0:T(8,128)(2,1)S(1)}, bf16[2,144,128]{2,1,0:T(8,128)(2,1)S(1)}, u32[]{:S(2)}, u32[]{:S(2)}) collective-permute-start(bf16[2,144,128]{2,1,0:T(8,128)(2,1)S(1)} %pad_maximum_fusion.11), channel_id=1, source_target_pairs={{0,20},{2,22},{4,16},{6,18},{8,28},{10,30},{12,24},{14,26},{16,4},... | collective-permute-start | bytes 221192 | tf_op jit(solution)/shard_map/ppermute | solution.py:329
  44.3 0.1 collective-permute-start.16
  44.4 2.4 %collective-permute-start.17 = (bf16[2,144,128]{2,1,0:T(8,128)(2,1)S(1)}, bf16[2,144,128]{2,1,0:T(8,128)(2,1)S(1)}, u32[]{:S(2)}, u32[]{:S(2)}) collective-permute-start(bf16[2,144,128]{2,1,0:T(8,128)(2,1)S(1)} %pad_maximum_fusion.13), channel_id=1, source_target_pairs={{0,28},{2,30},{4,24},{6,26},{8,20},{10,22},{12,16},{14,18},{16,12}... | collective-permute-start | bytes 221192 | tf_op jit(solution)/shard_map/ppermute | solution.py:329
  46.9 3.5 %collective-permute-done.15 = bf16[2,144,128]{2,1,0:T(8,128)(2,1)S(1)} collective-permute-done((bf16[2,144,128]{2,1,0:T(8,128)(2,1)S(1)}, bf16[2,144,128]{2,1,0:T(8,128)(2,1)S(1)}, u32[]{:S(2)}, u32[]{:S(2)}) %collective-permute-start.15) | collective-permute-done | bytes 73760 | tf_op jit(solution)/shard_map/ppermute | solution.py:329
  50.5 3.8 %collective-permute-done.16 = bf16[2,144,128]{2,1,0:T(8,128)(2,1)S(1)} collective-permute-done((bf16[2,144,128]{2,1,0:T(8,128)(2,1)S(1)}, bf16[2,144,128]{2,1,0:T(8,128)(2,1)S(1)}, u32[]{:S(2)}, u32[]{:S(2)}) %collective-permute-start.16) | collective-permute-done | bytes 73760 | tf_op jit(solution)/shard_map/ppermute | solution.py:329
  54.3 0.9 %shard_map.112.refs_0_ = bf16[10,144,128]{2,1,0:T(8,128)(2,1)S(1)} custom-call(s32[16]{0:T(128)S(1)} %copy-done.5, s32[16,10]{1,0:T(8,128)S(1)} %copy-done.4, bf16[8,2,144,128]{3,2,1,0:T(8,128)(2,1)S(1)} %bitcast_dynamic-update-slice_fusion.7.in_ref), custom_call_target="tpu_custom_call" | custom-call | tf_op jit(solution)/shard_map/pallas_call | solution.py:197
  55.2 0.1 collective-permute-done.17
  55.3 0.9 %shard_map.114.refs_1_ = bf16[10,144,128]{2,1,0:T(8,128)(2,1)S(1)} custom-call(s32[16]{0:T(128)S(1)} %copy-done.5, s32[16,10]{1,0:T(8,128)S(1)} %copy-done.4, bf16[8,2,144,128]{3,2,1,0:T(8,128)(2,1)S(1)} %bitcast_dynamic-update-slice_fusion.in_ref), custom_call_target="tpu_custom_call" | custom-call | tf_op jit(solution)/shard_map/pallas_call | solution.py:197
  56.3 1.6 %collective-permute-start.18 = (bf16[10,144,128]{2,1,0:T(8,128)(2,1)S(1)}, bf16[10,144,128]{2,1,0:T(8,128)(2,1)S(1)}, u32[]{:S(2)}, u32[]{:S(2)}) collective-permute-start(bf16[10,144,128]{2,1,0:T(8,128)(2,1)S(1)} %shard_map.112.refs_0_), channel_id=1, source_target_pairs={{0,1},{1,0},{2,3},{3,2},{4,5},{5,4},{6,7},{7,6},{8,9},{9,8},{10,11... | collective-permute-start | bytes 1105928 | tf_op jit(solution)/shard_map/ppermute | solution.py:324
  57.8 0.5 collective-permute-start.19
  58.4 0.2 reshape_squeeze.3
  58.6 0.1 fusion.2
  58.8 1.5 %copy.12 = bf16[32,32,640]{2,1,0:T(8,128)(2,1)} copy(bf16[32,32,640]{2,0,1:T(8,128)(2,1)S(1)} %fusion.2) | data formatting | bytes 2621440 | tf_op jit(solution)/shard_map/transpose | solution.py:357
  60.3 7.5 %collective-permute-done.18.refs_2_ = bf16[10,144,128]{2,1,0:T(8,128)(2,1)S(1)} collective-permute-done((bf16[10,144,128]{2,1,0:T(8,128)(2,1)S(1)}, bf16[10,144,128]{2,1,0:T(8,128)(2,1)S(1)}, u32[]{:S(2)}, u32[]{:S(2)}) %collective-permute-start.18) | collective-permute-done | bytes 368672 | tf_op jit(solution)/shard_map/ppermute | solution.py:324
  67.8 6.0 %collective-permute-done.19.refs_3_ = bf16[10,144,128]{2,1,0:T(8,128)(2,1)S(1)} collective-permute-done((bf16[10,144,128]{2,1,0:T(8,128)(2,1)S(1)}, bf16[10,144,128]{2,1,0:T(8,128)(2,1)S(1)}, u32[]{:S(2)}, u32[]{:S(2)}) %collective-permute-start.19) | collective-permute-done | bytes 368672 | tf_op jit(solution)/shard_map/ppermute | solution.py:324
  73.8 0.7 copy-done.10
  74.5 10.6 %shard_map.115 = (bf16[16,4096]{1,0:T(8,128)(2,1)}, bf16[16,4096]{1,0:T(8,128)(2,1)}) custom-call(s32[16]{0:T(128)} %dest_ref.9, s32[16]{0:T(128)} %len_ref.1, bf16[1024,640]{1,0:T(8,128)(2,1)} %bitcast.53, bf16[32,512,128]{2,1,0:T(8,128)(2,1)} %w_ref.1, bf16[10,144,128]{2,1,0:T(8,128)(2,1)} %copy-done, bf16[10,144,128]{2,1,0:T(8,128)(2,1)} %copy-done.1, ...), custom_call_target="tpu_custom_call" | custom-call | tf_op jit(solution)/shard_map/pallas_call | solution.py:295
  85.1 1.5 %collective-permute-start.20 = (bf16[16,4096]{1,0:T(8,128)(2,1)}, bf16[16,4096]{1,0:T(8,128)(2,1)S(1)}, u32[]{:S(2)}, u32[]{:S(2)}) collective-permute-start(bf16[16,4096]{1,0:T(8,128)(2,1)} %get-tuple-element.23), channel_id=1, source_target_pairs={{0,1},{1,0},{2,3},{3,2},{4,5},{5,4},{6,7},{7,6},{8,9},{9,8},{10,11... | collective-permute-start | bytes 393224 | tf_op jit(solution)/shard_map/ppermute | solution.py:324
  86.6 3.7 %collective-permute-done.20 = bf16[16,4096]{1,0:T(8,128)(2,1)S(1)} collective-permute-done((bf16[16,4096]{1,0:T(8,128)(2,1)}, bf16[16,4096]{1,0:T(8,128)(2,1)S(1)}, u32[]{:S(2)}, u32[]{:S(2)}) %collective-permute-start.20) | collective-permute-done | bytes 131104 | tf_op jit(solution)/shard_map/ppermute | solution.py:324
  90.3 0.9 %broadcast_select_fusion.1 = (bf16[16,4096]{1,0:T(8,128)(2,1)S(1)}, bf16[16,4096]{1,0:T(8,128)(2,1)S(1)}) fusion(bf16[16,4096]{1,0:T(8,128)(2,1)S(1)} %collective-permute-done.20, bf16[16,4096]{1,0:T(8,128)(2,1)} %get-tuple-element.24, pred[]{:T(512)S(6)} %eq.11, pred[]{:T(512)S(6)} %eq.12), kind=kLoop, calls=%fused_computation.6 | loop fusion | flops 131072 | bytes 524290 | tf_op jit(solution)/shard_map/jit(_where)/select_n | solution.py:387
  91.3 0.7 maximum_bitcast_fusion
  (64 shorter events, 0.5 us)
Async XLA Ops:
  4.0 10.2 %collective-permute-start = (f32[4,144,128]{2,1,0:T(8,128)}, f32[4,144,128]{2,1,0:T(8,128)S(1)}, u32[]{:S(2)}, u32[]{:S(2)}) collective-permute-start(f32[4,144,128]{2,1,0:T(8,128)} %bitcast.58), channel_id=1, source_target_pairs={{0,1},{1,0},{2,3},{3,2},{4,5},{5,4},{6,7},{7,6},{8,9},{9,8},{10,11... | collective-permute-start | bytes 884744 | tf_op jit(solution)/shard_map/ppermute | solution.py:324
  5.6 13.8 %collective-permute-start.9 = (f32[4,144,128]{2,1,0:T(8,128)}, f32[4,144,128]{2,1,0:T(8,128)S(1)}, u32[]{:S(2)}, u32[]{:S(2)}) collective-permute-start(f32[4,144,128]{2,1,0:T(8,128)} %bitcast.57), channel_id=1, source_target_pairs={{0,1},{1,0},{2,3},{3,2},{4,5},{5,4},{6,7},{7,6},{8,9},{9,8},{10,11... | collective-permute-start | bytes 884744 | tf_op jit(solution)/shard_map/ppermute | solution.py:324
  6.1 8.1 %copy-start.4 = (s32[16,10]{1,0:T(8,128)S(1)}, s32[16,10]{1,0:T(8,128)}, u32[]{:S(2)}) copy-start(s32[16,10]{1,0:T(8,128)} %table_ref.7) | copy-start | bytes 1924
  6.1 8.1 %copy-start.5 = (s32[16]{0:T(128)S(1)}, s32[16]{0:T(128)}, u32[]{:S(2)}) copy-start(s32[16]{0:T(128)} %dest_ref.9) | copy-start | bytes 196
  6.1 8.1 %copy-start.6 = (f32[512]{0:T(512)S(1)}, f32[512]{0:T(512)}, u32[]{:S(2)}) copy-start(f32[512]{0:T(512)} %param.14) | copy-start | bytes 6148
  6.1 8.1 %copy-start.7 = (f32[1,128]{1,0:T(1,128)S(1)}, f32[1,128]{1,0:T(1,128)}, u32[]{:S(2)}) copy-start(f32[1,128]{1,0:T(1,128)} %constant.44.clone.freq_ref) | copy-start | bytes 1540
  14.2 1.0 %copy-start.3 = (f32[1,4,144,128]{3,2,1,0:T(8,128)S(1)}, f32[1,4,144,128]{3,2,1,0:T(8,128)}, u32[]{:S(2)}) copy-start(f32[1,4,144,128]{3,2,1,0:T(8,128)} %get-tuple-element.15.own_ref) | copy-start | bytes 884740
  16.4 5.3 %collective-permute-start.1 = (bf16[8,144,128]{2,1,0:T(8,128)(2,1)S(1)}, bf16[8,144,128]{2,1,0:T(8,128)(2,1)S(1)}, u32[]{:S(2)}, u32[]{:S(2)}) collective-permute-start(bf16[8,144,128]{2,1,0:T(8,128)(2,1)S(1)} %get-tuple-element.18), channel_id=1, source_target_pairs={{0,2},{2,0},{4,6},{6,4},{8,10},{10,8},{12,14},{14,12},{16,18},{18,... | collective-permute-start | bytes 884744 | tf_op jit(solution)/shard_map/ppermute | solution.py:329
  19.4 1.0 %copy-start.2 = (f32[1,4,144,128]{3,2,1,0:T(8,128)S(1)}, f32[1,4,144,128]{3,2,1,0:T(8,128)}, u32[]{:S(2)}) copy-start(f32[1,4,144,128]{3,2,1,0:T(8,128)} %get-tuple-element.19.own_ref) | copy-start | bytes 884740
  21.6 4.3 %collective-permute-start.10 = (bf16[8,144,128]{2,1,0:T(8,128)(2,1)S(1)}, bf16[8,144,128]{2,1,0:T(8,128)(2,1)S(1)}, u32[]{:S(2)}, u32[]{:S(2)}) collective-permute-start(bf16[8,144,128]{2,1,0:T(8,128)(2,1)S(1)} %get-tuple-element.22), channel_id=1, source_target_pairs={{0,2},{2,0},{4,6},{6,4},{8,10},{10,8},{12,14},{14,12},{16,18},{18,... | collective-permute-start | bytes 884744 | tf_op jit(solution)/shard_map/ppermute | solution.py:329
  21.8 7.0 %collective-permute-start.2 = (bf16[2,144,128]{2,1,0:T(8,128)(2,1)S(1)}, bf16[2,144,128]{2,1,0:T(8,128)(2,1)S(1)}, u32[]{:S(2)}, u32[]{:S(2)}) collective-permute-start(bf16[2,144,128]{2,1,0:T(8,128)(2,1)S(1)} %pad_maximum_fusion), channel_id=1, source_target_pairs={{0,4},{2,6},{4,0},{6,2},{8,12},{10,14},{12,8},{14,10},{16,20},{18,... | collective-permute-start | bytes 221192 | tf_op jit(solution)/shard_map/ppermute | solution.py:329
  22.4 6.9 %collective-permute-start.3 = (bf16[2,144,128]{2,1,0:T(8,128)(2,1)S(1)}, bf16[2,144,128]{2,1,0:T(8,128)(2,1)S(1)}, u32[]{:S(2)}, u32[]{:S(2)}) collective-permute-start(bf16[2,144,128]{2,1,0:T(8,128)(2,1)S(1)} %pad_maximum_fusion.1), channel_id=1, source_target_pairs={{0,8},{2,10},{4,12},{6,14},{8,0},{10,2},{12,4},{14,6},{16,24},{18,... | collective-permute-start | bytes 221192 | tf_op jit(solution)/shard_map/ppermute | solution.py:329
  24.0 7.9 %collective-permute-start.4 = (bf16[2,144,128]{2,1,0:T(8,128)(2,1)S(1)}, bf16[2,144,128]{2,1,0:T(8,128)(2,1)S(1)}, u32[]{:S(2)}, u32[]{:S(2)}) collective-permute-start(bf16[2,144,128]{2,1,0:T(8,128)(2,1)S(1)} %pad_maximum_fusion.2), channel_id=1, source_target_pairs={{0,12},{2,14},{4,8},{6,10},{8,4},{10,6},{12,0},{14,2},{16,28},{18,... | collective-permute-start | bytes 221192 | tf_op jit(solution)/shard_map/ppermute | solution.py:329
  25.5 7.0 %collective-permute-start.5 = (bf16[2,144,128]{2,1,0:T(8,128)(2,1)S(1)}, bf16[2,144,128]{2,1,0:T(8,128)(2,1)S(1)}, u32[]{:S(2)}, u32[]{:S(2)}) collective-permute-start(bf16[2,144,128]{2,1,0:T(8,128)(2,1)S(1)} %pad_maximum_fusion.3), channel_id=1, source_target_pairs={{0,16},{2,18},{4,20},{6,22},{8,24},{10,26},{12,28},{14,30},{16,0},... | collective-permute-start | bytes 221192 | tf_op jit(solution)/shard_map/ppermute | solution.py:329
  26.0 12.2 %collective-permute-start.6 = (bf16[2,144,128]{2,1,0:T(8,128)(2,1)S(1)}, bf16[2,144,128]{2,1,0:T(8,128)(2,1)S(1)}, u32[]{:S(2)}, u32[]{:S(2)}) collective-permute-start(bf16[2,144,128]{2,1,0:T(8,128)(2,1)S(1)} %pad_maximum_fusion.4), channel_id=1, source_target_pairs={{0,20},{2,22},{4,16},{6,18},{8,28},{10,30},{12,24},{14,26},{16,4},... | collective-permute-start | bytes 221192 | tf_op jit(solution)/shard_map/ppermute | solution.py:329
  28.6 29.8 %copy-start.11 = (bf16[1,32,2048]{2,1,0:T(8,128)(2,1)S(1)}, bf16[1,32,2048]{2,1,0:T(8,128)(2,1)}, u32[]{:S(2)}) copy-start(bf16[1,32,2048]{2,1,0:T(8,128)(2,1)} %param.16) | copy-start | bytes 393220
  28.6 30.0 %copy-start.8 = (bf16[1,32,32,512]{3,2,1,0:T(8,128)(2,1)S(1)}, bf16[1,32,32,512]{3,2,1,0:T(8,128)(2,1)}, u32[]{:S(2)}) copy-start(bf16[1,32,32,512]{3,2,1,0:T(8,128)(2,1)} %param.15) | copy-start | bytes 3145732
  28.8 11.9 %collective-permute-start.7 = (bf16[2,144,128]{2,1,0:T(8,128)(2,1)S(1)}, bf16[2,144,128]{2,1,0:T(8,128)(2,1)S(1)}, u32[]{:S(2)}, u32[]{:S(2)}) collective-permute-start(bf16[2,144,128]{2,1,0:T(8,128)(2,1)S(1)} %pad_maximum_fusion.5), channel_id=1, source_target_pairs={{0,24},{2,26},{4,28},{6,30},{8,16},{10,18},{12,20},{14,22},{16,8},... | collective-permute-start | bytes 221192 | tf_op jit(solution)/shard_map/ppermute | solution.py:329
  29.3 12.0 %collective-permute-start.8 = (bf16[2,144,128]{2,1,0:T(8,128)(2,1)S(1)}, bf16[2,144,128]{2,1,0:T(8,128)(2,1)S(1)}, u32[]{:S(2)}, u32[]{:S(2)}) collective-permute-start(bf16[2,144,128]{2,1,0:T(8,128)(2,1)S(1)} %pad_maximum_fusion.6), channel_id=1, source_target_pairs={{0,28},{2,30},{4,24},{6,26},{8,20},{10,22},{12,16},{14,18},{16,12}... | collective-permute-start | bytes 221192 | tf_op jit(solution)/shard_map/ppermute | solution.py:329
  31.9 12.4 %collective-permute-start.11 = (bf16[2,144,128]{2,1,0:T(8,128)(2,1)S(1)}, bf16[2,144,128]{2,1,0:T(8,128)(2,1)S(1)}, u32[]{:S(2)}, u32[]{:S(2)}) collective-permute-start(bf16[2,144,128]{2,1,0:T(8,128)(2,1)S(1)} %pad_maximum_fusion.7), channel_id=1, source_target_pairs={{0,4},{2,6},{4,0},{6,2},{8,12},{10,14},{12,8},{14,10},{16,20},{18,... | collective-permute-start | bytes 221192 | tf_op jit(solution)/shard_map/ppermute | solution.py:329
  32.5 11.9 %collective-permute-start.12 = (bf16[2,144,128]{2,1,0:T(8,128)(2,1)S(1)}, bf16[2,144,128]{2,1,0:T(8,128)(2,1)S(1)}, u32[]{:S(2)}, u32[]{:S(2)}) collective-permute-start(bf16[2,144,128]{2,1,0:T(8,128)(2,1)S(1)} %pad_maximum_fusion.8), channel_id=1, source_target_pairs={{0,8},{2,10},{4,12},{6,14},{8,0},{10,2},{12,4},{14,6},{16,24},{18,... | collective-permute-start | bytes 221192 | tf_op jit(solution)/shard_map/ppermute | solution.py:329
  38.2 8.7 %collective-permute-start.13 = (bf16[2,144,128]{2,1,0:T(8,128)(2,1)S(1)}, bf16[2,144,128]{2,1,0:T(8,128)(2,1)S(1)}, u32[]{:S(2)}, u32[]{:S(2)}) collective-permute-start(bf16[2,144,128]{2,1,0:T(8,128)(2,1)S(1)} %pad_maximum_fusion.9), channel_id=1, source_target_pairs={{0,12},{2,14},{4,8},{6,10},{8,4},{10,6},{12,0},{14,2},{16,28},{18,... | collective-permute-start | bytes 221192 | tf_op jit(solution)/shard_map/ppermute | solution.py:329
  40.7 6.2 %collective-permute-start.14 = (bf16[2,144,128]{2,1,0:T(8,128)(2,1)S(1)}, bf16[2,144,128]{2,1,0:T(8,128)(2,1)S(1)}, u32[]{:S(2)}, u32[]{:S(2)}) collective-permute-start(bf16[2,144,128]{2,1,0:T(8,128)(2,1)S(1)} %pad_maximum_fusion.10), channel_id=1, source_target_pairs={{0,16},{2,18},{4,20},{6,22},{8,24},{10,26},{12,28},{14,30},{16,0},... | collective-permute-start | bytes 221192 | tf_op jit(solution)/shard_map/ppermute | solution.py:329
  41.3 9.1 %collective-permute-start.15 = (bf16[2,144,128]{2,1,0:T(8,128)(2,1)S(1)}, bf16[2,144,128]{2,1,0:T(8,128)(2,1)S(1)}, u32[]{:S(2)}, u32[]{:S(2)}) collective-permute-start(bf16[2,144,128]{2,1,0:T(8,128)(2,1)S(1)} %pad_maximum_fusion.11), channel_id=1, source_target_pairs={{0,20},{2,22},{4,16},{6,18},{8,28},{10,30},{12,24},{14,26},{16,4},... | collective-permute-start | bytes 221192 | tf_op jit(solution)/shard_map/ppermute | solution.py:329
  44.3 9.9 %collective-permute-start.16 = (bf16[2,144,128]{2,1,0:T(8,128)(2,1)S(1)}, bf16[2,144,128]{2,1,0:T(8,128)(2,1)S(1)}, u32[]{:S(2)}, u32[]{:S(2)}) collective-permute-start(bf16[2,144,128]{2,1,0:T(8,128)(2,1)S(1)} %pad_maximum_fusion.12), channel_id=1, source_target_pairs={{0,24},{2,26},{4,28},{6,30},{8,16},{10,18},{12,20},{14,22},{16,8},... | collective-permute-start | bytes 221192 | tf_op jit(solution)/shard_map/ppermute | solution.py:329
  44.4 10.9 %collective-permute-start.17 = (bf16[2,144,128]{2,1,0:T(8,128)(2,1)S(1)}, bf16[2,144,128]{2,1,0:T(8,128)(2,1)S(1)}, u32[]{:S(2)}, u32[]{:S(2)}) collective-permute-start(bf16[2,144,128]{2,1,0:T(8,128)(2,1)S(1)} %pad_maximum_fusion.13), channel_id=1, source_target_pairs={{0,28},{2,30},{4,24},{6,26},{8,20},{10,22},{12,16},{14,18},{16,12}... | collective-permute-start | bytes 221192 | tf_op jit(solution)/shard_map/ppermute | solution.py:329
  55.2 5.1 %copy-start = (bf16[10,144,128]{2,1,0:T(8,128)(2,1)}, bf16[10,144,128]{2,1,0:T(8,128)(2,1)S(1)}, u32[]{:S(2)}) copy-start(bf16[10,144,128]{2,1,0:T(8,128)(2,1)S(1)} %shard_map.112.refs_0_) | copy-start | bytes 1105924
  56.3 4.0 %copy-start.1 = (bf16[10,144,128]{2,1,0:T(8,128)(2,1)}, bf16[10,144,128]{2,1,0:T(8,128)(2,1)S(1)}, u32[]{:S(2)}) copy-start(bf16[10,144,128]{2,1,0:T(8,128)(2,1)S(1)} %shard_map.114.refs_1_) | copy-start | bytes 1105924
  56.3 11.5 %collective-permute-start.18 = (bf16[10,144,128]{2,1,0:T(8,128)(2,1)S(1)}, bf16[10,144,128]{2,1,0:T(8,128)(2,1)S(1)}, u32[]{:S(2)}, u32[]{:S(2)}) collective-permute-start(bf16[10,144,128]{2,1,0:T(8,128)(2,1)S(1)} %shard_map.112.refs_0_), channel_id=1, source_target_pairs={{0,1},{1,0},{2,3},{3,2},{4,5},{5,4},{6,7},{7,6},{8,9},{9,8},{10,11... | collective-permute-start | bytes 1105928 | tf_op jit(solution)/shard_map/ppermute | solution.py:324
  57.8 15.9 %collective-permute-start.19 = (bf16[10,144,128]{2,1,0:T(8,128)(2,1)S(1)}, bf16[10,144,128]{2,1,0:T(8,128)(2,1)S(1)}, u32[]{:S(2)}, u32[]{:S(2)}) collective-permute-start(bf16[10,144,128]{2,1,0:T(8,128)(2,1)S(1)} %shard_map.114.refs_1_), channel_id=1, source_target_pairs={{0,1},{1,0},{2,3},{3,2},{4,5},{5,4},{6,7},{7,6},{8,9},{9,8},{10,11... | collective-permute-start | bytes 1105928 | tf_op jit(solution)/shard_map/ppermute | solution.py:324
  67.8 6.0 %copy-start.9 = (bf16[10,144,128]{2,1,0:T(8,128)(2,1)}, bf16[10,144,128]{2,1,0:T(8,128)(2,1)S(1)}, u32[]{:S(2)}) copy-start(bf16[10,144,128]{2,1,0:T(8,128)(2,1)S(1)} %collective-permute-done.18.refs_2_) | copy-start | bytes 1105924
  73.8 0.7 copy-start.10
  85.1 5.2 %collective-permute-start.20 = (bf16[16,4096]{1,0:T(8,128)(2,1)}, bf16[16,4096]{1,0:T(8,128)(2,1)S(1)}, u32[]{:S(2)}, u32[]{:S(2)}) collective-permute-start(bf16[16,4096]{1,0:T(8,128)(2,1)} %get-tuple-element.23), channel_id=1, source_target_pairs={{0,1},{1,0},{2,3},{3,2},{4,5},{5,4},{6,7},{7,6},{8,9},{9,8},{10,11... | collective-permute-start | bytes 393224 | tf_op jit(solution)/shard_map/ppermute | solution.py:324
where the time goes:
time: 92.2 us; the launch traced here: 92 us
  waiting for transfers between devices  32 us (35%)
  starting transfers between devices  29.9 us (32%)
  Pallas kernels  23.1 us (25%)
  local copies, waits for them, and re-layouts  4.74 us (5%)
  other arithmetic  1.91 us (2%)
    ppermute x16, starting transfers between devices, trade(): return lax.ppermute(value, 'tok', [(i, i ^ mask) for i in range(count)])  24.1 us
    ppermute x5, waiting for transfers between devices, shift(): lax.ppermute(value, axis, [(i, (i + by) % count) for i in range(count)])  24 us
    pallas_call x1, Pallas kernels, attend(): pl.pallas_call(functools.partial(attend_kernel, planes=planes, chunks=chu...  10.6 us
    pallas_call x2, Pallas kernels, project(): pl.pallas_call(functools.partial(project_kernel, chunks=chunks, pages=pag...  8.05 us
    ppermute x16, waiting for transfers between devices, trade(): return lax.ppermute(value, 'tok', [(i, i ^ mask) for i in range(count)])  8.02 us
    ppermute x5, starting transfers between devices, shift(): lax.ppermute(value, axis, [(i, (i + by) % count) for i in range(count)])  5.72 us
    unnamed x36, local copies, waits for them, and re-layouts  2.87 us
    pallas_call x2, Pallas kernels, finish(): pl.pallas_call(functools.partial(finish_kernel, tokens=tokens, blocks=blo...  2.58 us
  transfers between devices with their start and end apart: 21, of which 9 were waited for; matrix products, arithmetic and copies ran while one was open for 2% of the time, Pallas kernels for 8%

commit v1 on v0

--- a/solution.py
+++ b/solution.py
@@ -20,6 +20,7 @@
 
 
 MIB = 1024 * 1024
+PART_MIB, END_MIB = 24, 24
 
 
 def params(mib):
@@ -77,7 +78,7 @@
                 )
 
 
-def project(hidden, w_latent, w_rope, shares, head_count, chunks):
+def project(hidden, w_latent, w_rope, shares, head_count, chunks, keep=False):
     features = hidden.shape[1]
     pages = hidden.shape[0] // PAGE
     share = PAGE // head_count
@@ -102,7 +103,7 @@
             pltpu.VMEM(side.shape, BF16),
             pltpu.SemaphoreType.DMA((2 + count, parts)),
         ],
-        compiler_params=params(63),
+        compiler_params=params(63 if count > 1 or not keep else 62),
         cost_estimate=pl.CostEstimate(
             flops=flops,
             bytes_accessed=2 * features * (count * pages * share + w_latent.shape[1] + LANES),
@@ -204,62 +205,67 @@
 
 
 def fold(value, op):
-    width = value.shape[1]
-    while width > LANES and width % (2 * LANES) == 0:
-        width //= 2
-        value = op(value[:, :width], value[:, width:])
-    return value
-
-
-def attend_kernel(
-    dest_ref, len_ref, q_ref, w_ref, *refs, planes, chunks, tokens, blocks, rows_q, step
-):
-    payloads = refs[: planes * chunks]
-    outs = refs[planes * chunks : planes * (chunks + 1)]
-    key_ref, score_ref, acc_ref, top_ref, sum_ref, map_ref, w_buf, w_sem = refs[planes * (chunks + 1) :]
-    w_copy = pltpu.make_async_copy(w_ref, w_buf, w_sem)
-    w_copy.start()
+    parts = [value[:, at : at + LANES] for at in range(0, value.shape[1], LANES)]
+    while len(parts) > 1:
+        pairs = [op(x, y) for x, y in zip(parts[::2], parts[1::2])]
+        parts = pairs + parts[len(pairs) * 2 :]
+    return parts[0]
+
+
+def fill_keys(key_ref, payloads, tokens, width):
+    region = payloads[0].shape[0] * tokens
+    for n, payload in enumerate(payloads):
+        def fill(slot, _, n=n, payload=payload):
+            at = pl.multiple_of(n * region + slot * tokens, tokens)
+            for b in range(width // LANES):
+                key_ref[pl.ds(at, tokens), b * LANES : (b + 1) * LANES] = payload[
+                    slot, b * tokens : (b + 1) * tokens
+                ]
+            packed = payload[slot, width * tokens // LANES :].astype(F32)
+            swapped = pltpu.roll(packed, 64, 1)
+            key_ref[pl.ds(at, tokens), width:] = jnp.concatenate([packed, swapped], axis=0).astype(BF16)
+            return 0
+
+        lax.fori_loop(0, payload.shape[0], fill, 0)
+    used = len(payloads) * region
+    if used < key_ref.shape[0]:
+        key_ref[used:] = jnp.zeros_like(key_ref[used:])
+
+
+def dead_bias(at, step, context, slots, tokens, offsets):
+    row = at + lax.broadcasted_iota(jnp.int32, (1, step), 1)
+    region = slots * tokens
+    position = jnp.full((1, step), slots * PAGE, jnp.int32)
+    for n, offset in enumerate(offsets):
+        rest = row - n * region
+        inside = (rest // tokens) * PAGE + offset + rest % tokens
+        position = jnp.where((rest >= 0) & (rest < region), inside, position)
+    return jnp.where(position < context, 0.0, FLOOR)
+
+
+def payload_offsets(origins, planes, chunks, tokens):
     head = lax.axis_index("head")
-    context = len_ref[request_of(dest_ref, lax.axis_index("tok"))]
-    share = tokens * chunks
-    width = blocks * LANES
-    count = q_ref.shape[0]
-    steps = lax.div(context + (step - 1), step)
-    live = steps * (step // PAGE)
-
-    for plane in range(planes):
-        for chunk in range(chunks):
-            payload = payloads[plane * chunks + chunk]
-            offset = lax.rem(head + (planes - plane), planes) * share + chunk * tokens
-
-            def fill(slot, _, payload=payload, offset=offset):
-                at = pl.multiple_of(slot * PAGE + offset, tokens)
-                for b in range(blocks):
-                    key_ref[pl.ds(at, tokens), b * LANES : (b + 1) * LANES] = payload[
-                        slot, b * tokens : (b + 1) * tokens
-                    ]
-                packed = payload[slot, width * tokens // LANES :].astype(F32)
-                swapped = pltpu.roll(packed, 64, 1)
-                key_ref[pl.ds(at, tokens), width:] = jnp.concatenate([packed, swapped], axis=0).astype(BF16)
-                return 0
-
-            lax.fori_loop(0, live, fill, 0)
-
-    top_ref[...] = jnp.full_like(top_ref, FLOOR)
+    return [
+        lax.rem(head + (planes - behind), planes) * (tokens * chunks) + chunk * tokens
+        for behind, chunk in origins
+    ]
+
+
+def score_keys(q_ref, key_ref, score_ref, top_ref, bias_of):
+    blocks, _, step = score_ref.shape
 
     def score_step(i, _):
         at = pl.multiple_of(i * step, step)
-        scores = nt_dot(q_ref[...], key_ref[pl.ds(at, step)])
-        position = at + lax.broadcasted_iota(jnp.int32, (1, step), 1)
-        scores = scores + jnp.where(position < context, 0.0, FLOOR)
+        scores = nt_dot(q_ref[...], key_ref[pl.ds(at, step)]) + bias_of(at, step)
         score_ref[i] = scores
         top_ref[...] = jnp.maximum(top_ref[...], fold(scores, jnp.maximum))
         return 0
 
-    lax.fori_loop(0, steps, score_step, 0)
-    top = jnp.max(top_ref[...], axis=1, keepdims=True)
-    acc_ref[...] = jnp.zeros_like(acc_ref)
-    sum_ref[...] = jnp.zeros_like(sum_ref)
+    lax.fori_loop(0, blocks, score_step, 0)
+
+
+def weigh_keys(key_ref, score_ref, acc_ref, sum_ref, top, width):
+    blocks, _, step = score_ref.shape
 
     def value_step(i, _):
         at = pl.multiple_of(i * step, step)
@@ -270,7 +276,68 @@
         sum_ref[...] += fold(weights, jnp.add)
         return 0
 
-    lax.fori_loop(0, steps, value_step, 0)
+    lax.fori_loop(0, blocks, value_step, 0)
+
+
+def start_state(acc_ref, top_ref, sum_ref, carried, top_of):
+    if not carried:
+        top_ref[...] = jnp.full_like(top_ref, FLOOR)
+    else:
+        top_ref[...] = carried[1][...]
+    top_of()
+    top = jnp.max(top_ref[...], axis=1, keepdims=True)
+    if not carried:
+        acc_ref[...] = jnp.zeros_like(acc_ref)
+        sum_ref[...] = jnp.zeros_like(sum_ref)
+    else:
+        factor = jnp.exp2((carried[1][:, :1] - top) * (SCALE * LOG2E))
+        acc_ref[...] = carried[0][...] * factor
+        sum_ref[...] = carried[2][...] * factor
+    return top
+
+
+def part_kernel(dest_ref, len_ref, q_ref, *refs, carry, origins, planes, chunks, tokens, width):
+    carried, refs = refs[:carry], refs[carry:]
+    payloads = refs[: len(origins)]
+    acc_ref, top_ref, sum_ref, key_ref, score_ref = refs[len(origins) :]
+    context = len_ref[request_of(dest_ref, lax.axis_index("tok"))]
+    offsets = payload_offsets(origins, planes, chunks, tokens)
+    slots = payloads[0].shape[0]
+    fill_keys(key_ref, payloads, tokens, width)
+    top = start_state(
+        acc_ref, top_ref, sum_ref, carried,
+        lambda: score_keys(
+            q_ref, key_ref, score_ref, top_ref,
+            lambda at, step: dead_bias(at, step, context, slots, tokens, offsets),
+        ),
+    )
+    top_ref[...] = jnp.broadcast_to(top, top_ref.shape)
+    weigh_keys(key_ref, score_ref, acc_ref, sum_ref, top, width)
+
+
+def end_kernel(
+    dest_ref, len_ref, q_ref, w_ref, acc0_ref, top0_ref, sum0_ref, *refs,
+    origins, planes, chunks, tokens, width, rows_q,
+):
+    payloads = refs[: len(origins)]
+    outs = refs[len(origins) : len(origins) + planes]
+    key_ref, score_ref, acc_ref, top_ref, sum_ref, map_ref, w_buf, w_sem = refs[len(origins) + planes :]
+    w_copy = pltpu.make_async_copy(w_ref, w_buf, w_sem)
+    w_copy.start()
+    head = lax.axis_index("head")
+    context = len_ref[request_of(dest_ref, lax.axis_index("tok"))]
+    offsets = payload_offsets(origins, planes, chunks, tokens)
+    slots = payloads[0].shape[0]
+    count = q_ref.shape[0]
+    fill_keys(key_ref, payloads, tokens, width)
+    top = start_state(
+        acc_ref, top_ref, sum_ref, (acc0_ref, top0_ref, sum0_ref),
+        lambda: score_keys(
+            q_ref, key_ref, score_ref, top_ref,
+            lambda at, step: dead_bias(at, step, context, slots, tokens, offsets),
+        ),
+    )
+    weigh_keys(key_ref, score_ref, acc_ref, sum_ref, top, width)
     owned = rows_q // planes
     inverse = 1.0 / jnp.sum(sum_ref[...], axis=1, keepdims=True)
     w_copy.wait()
@@ -284,39 +351,84 @@
         outs[d][...] = map_ref[lax.rem(head + d, planes)].astype(BF16)
 
 
-def attend(dest, ctx_len, query, w_value, payloads, planes, chunks, tokens):
+def key_scratch(payloads, tokens, count, lat):
+    used = len(payloads) * payloads[0].shape[0] * tokens
+    step = 256 if used > 512 else (used + LANES - 1) // LANES * LANES
+    keys = (used + step - 1) // step * step
+    return [pltpu.VMEM((keys, lat + LANES), BF16), pltpu.VMEM((keys // step, count, step), F32)]
+
+
+def attend_part(dest, ctx_len, query, lat, payloads, carried, planes, chunks, tokens):
+    count = query.shape[0]
+    vmem, smem = pl.BlockSpec(memory_space=pltpu.VMEM), pl.BlockSpec(memory_space=pltpu.SMEM)
+    state = [(count, lat), (count, LANES), (count, LANES)]
+    return pl.pallas_call(
+        functools.partial(
+            part_kernel,
+            carry=len(carried),
+            origins=tuple(payloads),
+            planes=planes,
+            chunks=chunks,
+            tokens=tokens,
+            width=lat,
+        ),
+        in_specs=[smem, smem, vmem] + [vmem] * (len(carried) + len(payloads)),
+        out_specs=[vmem] * 3,
+        out_shape=[jax.ShapeDtypeStruct(shape, F32) for shape in state],
+        scratch_shapes=key_scratch(list(payloads.values()), tokens, count, lat),
+        compiler_params=params(PART_MIB),
+    )(dest, ctx_len, query, *carried, *payloads.values())
+
+
+def attend_end(dest, ctx_len, query, w_value, payloads, carried, planes, chunks, tokens):
     heads, lat, _ = w_value.shape
     count = query.shape[0]
     rows_q = count // heads
-    slots = payloads[0].shape[0]
-    step = 2 * PAGE if slots % 2 == 0 else PAGE
-    keys = slots * PAGE
     vmem, smem = pl.BlockSpec(memory_space=pltpu.VMEM), pl.BlockSpec(memory_space=pltpu.SMEM)
+    state = [(count, lat), (count, LANES), (count, LANES)]
     return pl.pallas_call(
         functools.partial(
-            attend_kernel,
+            end_kernel,
+            origins=tuple(payloads),
             planes=planes,
             chunks=chunks,
             tokens=tokens,
-            blocks=lat // LANES,
+            width=lat,
             rows_q=rows_q,
-            step=step,
         ),
-        in_specs=[smem, smem, vmem, pl.BlockSpec(memory_space=pltpu.HBM)] + [vmem] * len(payloads),
+        in_specs=[smem, smem, vmem, pl.BlockSpec(memory_space=pltpu.HBM)] + [vmem] * (3 + len(payloads)),
         out_specs=[vmem] * planes,
         out_shape=[jax.ShapeDtypeStruct((rows_q // planes, heads * LANES), BF16)] * planes,
-        scratch_shapes=[
-            pltpu.VMEM((keys, lat + LANES), BF16),
-            pltpu.VMEM((keys // step, count, step), F32),
-            pltpu.VMEM((count, lat), F32),
-            pltpu.VMEM((count, LANES), F32),
-            pltpu.VMEM((count, LANES), F32),
+        scratch_shapes=key_scratch(list(payloads.values()), tokens, count, lat)
+        + [pltpu.VMEM(shape, F32) for shape in state]
+        + [
             pltpu.VMEM((planes, rows_q // planes, heads * LANES), F32),
             pltpu.VMEM(w_value.shape, BF16),
             pltpu.SemaphoreType.DMA,
         ],
-        compiler_params=params(60),
-    )(dest, ctx_len, query, w_value, *payloads)
+        compiler_params=params(END_MIB),
+    )(dest, ctx_len, query, w_value, *carried, *payloads.values())
+
+
+def place_kernel(*refs):
+    out_ref, pieces = refs[-1], refs[:-1]
+    head, planes = lax.axis_index("head"), len(pieces)
+    width = pieces[0].shape[1]
+    for d, piece in enumerate(pieces):
+        first = pl.multiple_of(lax.rem(head + (planes - d), planes) * width, width)
+        out_ref[:, pl.ds(first, width)] = piece[...]
+
+
+def place(pieces):
+    vmem = pl.BlockSpec(memory_space=pltpu.VMEM)
+    rows, width = pieces[0].shape
+    return pl.pallas_call(
+        place_kernel,
+        in_specs=[vmem] * len(pieces),
+        out_specs=vmem,
+        out_shape=jax.ShapeDtypeStruct((rows, width * len(pieces)), BF16),
+        compiler_params=params(8),
+    )(*pieces)
 
 
 def shift(value, axis, by):
@@ -349,7 +461,7 @@
     arrived = []
     for c in range(chunks):
         arrived.append([shift(sent[c][d - 1], "head", d) for d in range(1, planes)])
-    own = project(hidden, w_latent, w_rope, my_head[None].astype(jnp.int32), planes, chunks)
+    own = project(hidden, w_latent, w_rope, my_head[None].astype(jnp.int32), planes, chunks, True)
 
     rows_q, heads = q_latent.shape[1], q_latent.shape[2]
     query_side = q_rope[0].reshape(rows_q, heads, rope_width)
@@ -372,21 +484,21 @@
         for k in range(1, groups // 2):
             landed.append(trade(jnp.stack([mine[k], got[k]]), 2 * k))
         picked.append(select(dest_group, page_table, jnp.stack(landed), pages))
-    payloads = list(picked)
-    for d in range(1, planes):
-        for c in range(chunks):
-            payloads.append(shift(picked[c], "head", d))
-    mapped = attend(dest_group, ctx_len, query, w_value, payloads, planes, chunks, tokens)
+    sent_keys = []
+    for c in range(chunks):
+        sent_keys.append({(d, c): shift(picked[c], "head", d) for d in range(1, planes)})
+    carried = ()
+    for c in range(chunks):
+        local = {(0, c): picked[c], **(sent_keys[c - 1] if c > 0 else {})}
+        carried = attend_part(
+            dest_group, ctx_len, query, w_value.shape[1], local, carried, planes, chunks, tokens
+        )
+    mapped = attend_end(
+        dest_group, ctx_len, query, w_value, sent_keys[-1], carried, planes, chunks, tokens
+    )
 
     pieces = [mapped[0]] + [shift(mapped[d], "head", d) for d in range(1, planes)]
-    columns = []
-    for source in range(planes):
-        behind = (my_head - source) % planes
-        column = pieces[0]
-        for d in range(1, planes):
-            column = jnp.where(behind == d, pieces[d], column)
-        columns.append(column)
-    return jnp.concatenate(columns, axis=1)[None]
+    return place(pieces)[None]
 
 
 def solution(mesh):

time: 92.2 us -> 108 us (1.17)
  the two profiles are of different devices: /device:TPU:20 before, /device:TPU:0 now
where the time goes in v1:
time: 108 us
  waiting for transfers between devices  54.2 us (50%)
  Pallas kernels  27.7 us (26%)
  starting transfers between devices  22 us (20%)
  local copies, waits for them, and re-layouts  3 us (3%)
    ppermute x16, waiting for transfers between devices, trade(): return lax.ppermute(value, 'tok', [(i, i ^ mask) for i in range(count)])  42.8 us
    ppermute x16, starting transfers between devices, trade(): return lax.ppermute(value, 'tok', [(i, i ^ mask) for i in range(count)])  15.2 us
    ppermute x5, waiting for transfers between devices, shift(): lax.ppermute(value, axis, [(i, (i + by) % count) for i in range(count)])  11.5 us
    pallas_call x2, Pallas kernels, attend_part(): pl.pallas_call(functools.partial(part_kernel, carry=len(carried), origins...  8.92 us
    pallas_call x2, Pallas kernels, project(): pl.pallas_call(functools.partial(project_kernel, chunks=chunks, pages=pag...  8.02 us
    ppermute x5, starting transfers between devices, shift(): lax.ppermute(value, axis, [(i, (i + by) % count) for i in range(count)])  6.83 us
    pallas_call x1, Pallas kernels, attend_end(): pl.pallas_call(functools.partial(end_kernel, origins=tuple(payloads), pla...  5.39 us
    pallas_call x2, Pallas kernels, finish(): pl.pallas_call(functools.partial(finish_kernel, tokens=tokens, blocks=blo...  2.76 us
  transfers between devices with their start and end apart: 21, of which 11 were waited for; matrix products, arithmetic and copies ran while one was open for 1% of the time, Pallas kernels for 16%

profile of v1, /device:TPU:0, one launch (start us, length us, event | category | flops | bytes accessed | tf_op | source)
XLA Modules:
  0.0 107.6 jit_solution(9723133348684472667)
XLA Ops:
  0.0 4.0 %shard_map.110 = (f32[1,4,144,128]{3,2,1,0:T(8,128)}, f32[1,4,144,128]{3,2,1,0:T(8,128)}) custom-call(s32[1]{0:T(128)S(6)} %select_n.7.share_ref, bf16[4,2,64,2560]{3,2,1,0:T(8,128)(2,1)} %bitcast.53, bf16[2560,512]{1,0:T(8,128)(2,1)} %wl_ref.3, bf16[64,2560]{1,0:T(8,128)(2,1)} %bitcast.55), custom_call_target="tpu_custom_call" | custom-call | flops 754974720 | bytes 4587520 | tf_op jit(solution)/shard_map/pallas_call | solution.py:93
  4.0 3.0 %collective-permute-start.9 = (f32[4,144,128]{2,1,0:T(8,128)}, f32[4,144,128]{2,1,0:T(8,128)S(1)}, u32[]{:S(2)}, u32[]{:S(2)}) collective-permute-start(f32[4,144,128]{2,1,0:T(8,128)} %bitcast.59), channel_id=1, source_target_pairs={{0,1},{1,0},{2,3},{3,2},{4,5},{5,4},{6,7},{7,6},{8,9},{9,8},{10,11... | collective-permute-start | bytes 884744 | tf_op jit(solution)/shard_map/ppermute | solution.py:436
  7.0 0.1 collective-permute-start
  7.1 4.0 %shard_map.109 = (f32[1,4,144,128]{3,2,1,0:T(8,128)}, f32[1,4,144,128]{3,2,1,0:T(8,128)}) custom-call(s32[1]{0:T(128)} %bitcast.4.share_ref, bf16[4,2,64,2560]{3,2,1,0:T(8,128)(2,1)} %bitcast.54, bf16[2560,512]{1,0:T(8,128)(2,1)} %wl_ref.3, bf16[64,2560]{1,0:T(8,128)(2,1)} %bitcast.56), custom_call_target="tpu_custom_call" | custom-call | flops 754974720 | bytes 4587520 | tf_op jit(solution)/shard_map/pallas_call | solution.py:93
  11.2 3.9 %collective-permute-done.9.refs_0_ = f32[4,144,128]{2,1,0:T(8,128)S(1)} collective-permute-done((f32[4,144,128]{2,1,0:T(8,128)}, f32[4,144,128]{2,1,0:T(8,128)S(1)}, u32[]{:S(2)}, u32[]{:S(2)}) %collective-permute-start.9) | collective-permute-done | bytes 294944 | tf_op jit(solution)/shard_map/ppermute | solution.py:436
  15.1 1.0 copy-done.2
  16.1 1.3 %shard_map.114 = (bf16[8,144,128]{2,1,0:T(8,128)(2,1)S(1)}, bf16[8,144,128]{2,1,0:T(8,128)(2,1)S(1)}) custom-call(s32[16]{0:T(128)S(1)} %copy-done.4, s32[16,10]{1,0:T(8,128)S(1)} %copy-done.3, f32[4,128]{1,0:T(4,128)S(1)} %bitcast.51, f32[1,128]{1,0:T(1,128)S(1)} %copy-done.7, f32[1,4,144,128]{3,2,1,0:T(8,128)S(1)} %copy-done.2, ...), custom_call_target="tpu_custom_call" | custom-call | tf_op jit(solution)/shard_map/pallas_call | solution.py:175
  17.4 0.1 collective-permute-start.10
  17.5 3.1 %collective-permute-done.refs_0_ = f32[4,144,128]{2,1,0:T(8,128)S(1)} collective-permute-done((f32[4,144,128]{2,1,0:T(8,128)}, f32[4,144,128]{2,1,0:T(8,128)S(1)}, u32[]{:S(2)}, u32[]{:S(2)}) %collective-permute-start) | collective-permute-done | bytes 294944 | tf_op jit(solution)/shard_map/ppermute | solution.py:436
  20.6 1.0 copy-done.1
  21.5 1.5 %shard_map.111 = (bf16[8,144,128]{2,1,0:T(8,128)(2,1)S(1)}, bf16[8,144,128]{2,1,0:T(8,128)(2,1)S(1)}) custom-call(s32[16]{0:T(128)S(1)} %copy-done.4, s32[16,10]{1,0:T(8,128)S(1)} %copy-done.3, f32[4,128]{1,0:T(4,128)S(1)} %bitcast.52, f32[1,128]{1,0:T(1,128)S(1)} %copy-done.7, f32[1,4,144,128]{3,2,1,0:T(8,128)S(1)} %copy-done.1, ...), custom_call_target="tpu_custom_call" | custom-call | tf_op jit(solution)/shard_map/pallas_call | solution.py:175
  23.0 0.1 collective-permute-start.1
  23.2 1.8 %collective-permute-start.11 = (bf16[2,144,128]{2,1,0:T(8,128)(2,1)S(1)}, bf16[2,144,128]{2,1,0:T(8,128)(2,1)S(1)}, u32[]{:S(2)}, u32[]{:S(2)}) collective-permute-start(bf16[2,144,128]{2,1,0:T(8,128)(2,1)S(1)} %pad_maximum_fusion.7), channel_id=1, source_target_pairs={{0,4},{2,6},{4,0},{6,2},{8,12},{10,14},{12,8},{14,10},{16,20},{18,... | collective-permute-start | bytes 221192 | tf_op jit(solution)/shard_map/ppermute | solution.py:441
  25.0 1.6 %collective-permute-start.12 = (bf16[2,144,128]{2,1,0:T(8,128)(2,1)S(1)}, bf16[2,144,128]{2,1,0:T(8,128)(2,1)S(1)}, u32[]{:S(2)}, u32[]{:S(2)}) collective-permute-start(bf16[2,144,128]{2,1,0:T(8,128)(2,1)S(1)} %pad_maximum_fusion.8), channel_id=1, source_target_pairs={{0,8},{2,10},{4,12},{6,14},{8,0},{10,2},{12,4},{14,6},{16,24},{18,... | collective-permute-start | bytes 221192 | tf_op jit(solution)/shard_map/ppermute | solution.py:441
  26.7 0.2 collective-permute-start.13
  26.9 2.9 %collective-permute-start.14 = (bf16[2,144,128]{2,1,0:T(8,128)(2,1)S(1)}, bf16[2,144,128]{2,1,0:T(8,128)(2,1)S(1)}, u32[]{:S(2)}, u32[]{:S(2)}) collective-permute-start(bf16[2,144,128]{2,1,0:T(8,128)(2,1)S(1)} %pad_maximum_fusion.10), channel_id=1, source_target_pairs={{0,16},{2,18},{4,20},{6,22},{8,24},{10,26},{12,28},{14,30},{16,0},... | collective-permute-start | bytes 221192 | tf_op jit(solution)/shard_map/ppermute | solution.py:441
  29.9 1.4 %collective-permute-start.15 = (bf16[2,144,128]{2,1,0:T(8,128)(2,1)S(1)}, bf16[2,144,128]{2,1,0:T(8,128)(2,1)S(1)}, u32[]{:S(2)}, u32[]{:S(2)}) collective-permute-start(bf16[2,144,128]{2,1,0:T(8,128)(2,1)S(1)} %pad_maximum_fusion.11), channel_id=1, source_target_pairs={{0,20},{2,22},{4,16},{6,18},{8,28},{10,30},{12,24},{14,26},{16,4},... | collective-permute-start | bytes 221192 | tf_op jit(solution)/shard_map/ppermute | solution.py:441
  31.4 0.0 copy-start.9
  31.4 3.7 %collective-permute-start.16 = (bf16[2,144,128]{2,1,0:T(8,128)(2,1)S(1)}, bf16[2,144,128]{2,1,0:T(8,128)(2,1)S(1)}, u32[]{:S(2)}, u32[]{:S(2)}) collective-permute-start(bf16[2,144,128]{2,1,0:T(8,128)(2,1)S(1)} %pad_maximum_fusion.12), channel_id=1, source_target_pairs={{0,24},{2,26},{4,28},{6,30},{8,16},{10,18},{12,20},{14,22},{16,8},... | collective-permute-start | bytes 221192 | tf_op jit(solution)/shard_map/ppermute | solution.py:441
  35.1 0.6 collective-permute-start.2
  35.7 4.8 %collective-permute-done.2 = bf16[2,144,128]{2,1,0:T(8,128)(2,1)S(1)} collective-permute-done((bf16[2,144,128]{2,1,0:T(8,128)(2,1)S(1)}, bf16[2,144,128]{2,1,0:T(8,128)(2,1)S(1)}, u32[]{:S(2)}, u32[]{:S(2)}) %collective-permute-start.2) | collective-permute-done | bytes 73760 | tf_op jit(solution)/shard_map/ppermute | solution.py:441
  40.6 4.6 %collective-permute-done.3 = bf16[2,144,128]{2,1,0:T(8,128)(2,1)S(1)} collective-permute-done((bf16[2,144,128]{2,1,0:T(8,128)(2,1)S(1)}, bf16[2,144,128]{2,1,0:T(8,128)(2,1)S(1)}, u32[]{:S(2)}, u32[]{:S(2)}) %collective-permute-start.3) | collective-permute-done | bytes 73760 | tf_op jit(solution)/shard_map/ppermute | solution.py:441
  45.1 0.5 collective-permute-start.4
  45.7 5.4 %collective-permute-done.4 = bf16[2,144,128]{2,1,0:T(8,128)(2,1)S(1)} collective-permute-done((bf16[2,144,128]{2,1,0:T(8,128)(2,1)S(1)}, bf16[2,144,128]{2,1,0:T(8,128)(2,1)S(1)}, u32[]{:S(2)}, u32[]{:S(2)}) %collective-permute-start.4) | collective-permute-done | bytes 73760 | tf_op jit(solution)/shard_map/ppermute | solution.py:441
  51.1 5.2 %collective-permute-done.5 = bf16[2,144,128]{2,1,0:T(8,128)(2,1)S(1)} collective-permute-done((bf16[2,144,128]{2,1,0:T(8,128)(2,1)S(1)}, bf16[2,144,128]{2,1,0:T(8,128)(2,1)S(1)}, u32[]{:S(2)}, u32[]{:S(2)}) %collective-permute-start.5) | collective-permute-done | bytes 73760 | tf_op jit(solution)/shard_map/ppermute | solution.py:441
  56.4 0.7 collective-permute-start.6
  57.1 6.7 %collective-permute-done.6 = bf16[2,144,128]{2,1,0:T(8,128)(2,1)S(1)} collective-permute-done((bf16[2,144,128]{2,1,0:T(8,128)(2,1)S(1)}, bf16[2,144,128]{2,1,0:T(8,128)(2,1)S(1)}, u32[]{:S(2)}, u32[]{:S(2)}) %collective-permute-start.6) | collective-permute-done | bytes 73760 | tf_op jit(solution)/shard_map/ppermute | solution.py:441
  63.8 6.1 %collective-permute-done.7 = bf16[2,144,128]{2,1,0:T(8,128)(2,1)S(1)} collective-permute-done((bf16[2,144,128]{2,1,0:T(8,128)(2,1)S(1)}, bf16[2,144,128]{2,1,0:T(8,128)(2,1)S(1)}, u32[]{:S(2)}, u32[]{:S(2)}) %collective-permute-start.7) | collective-permute-done | bytes 73760 | tf_op jit(solution)/shard_map/ppermute | solution.py:441
  70.0 0.8 collective-permute-start.8
  70.8 6.2 %collective-permute-done.8 = bf16[2,144,128]{2,1,0:T(8,128)(2,1)S(1)} collective-permute-done((bf16[2,144,128]{2,1,0:T(8,128)(2,1)S(1)}, bf16[2,144,128]{2,1,0:T(8,128)(2,1)S(1)}, u32[]{:S(2)}, u32[]{:S(2)}) %collective-permute-start.8) | collective-permute-done | bytes 73760 | tf_op jit(solution)/shard_map/ppermute | solution.py:441
  77.0 0.8 collective-permute-start.17
  77.8 0.9 shard_map.112.refs_0_
  78.8 1.6 %collective-permute-start.18 = (bf16[10,144,128]{2,1,0:T(8,128)(2,1)S(1)}, bf16[10,144,128]{2,1,0:T(8,128)(2,1)S(1)}, u32[]{:S(2)}, u32[]{:S(2)}) collective-permute-start(bf16[10,144,128]{2,1,0:T(8,128)(2,1)S(1)} %shard_map.112.refs_0_), channel_id=1, source_target_pairs={{0,1},{1,0},{2,3},{3,2},{4,5},{5,4},{6,7},{7,6},{8,9},{9,8},{10,11... | collective-permute-start | bytes 1105928 | tf_op jit(solution)/shard_map/ppermute | solution.py:436
  80.5 3.6 %collective-permute-done.17 = bf16[2,144,128]{2,1,0:T(8,128)(2,1)S(1)} collective-permute-done((bf16[2,144,128]{2,1,0:T(8,128)(2,1)S(1)}, bf16[2,144,128]{2,1,0:T(8,128)(2,1)S(1)}, u32[]{:S(2)}, u32[]{:S(2)}) %collective-permute-start.17) | collective-permute-done | bytes 73760 | tf_op jit(solution)/shard_map/ppermute | solution.py:441
  84.1 0.9 shard_map.115.refs_3_
  85.0 1.6 %collective-permute-start.19 = (bf16[10,144,128]{2,1,0:T(8,128)(2,1)S(1)}, bf16[10,144,128]{2,1,0:T(8,128)(2,1)S(1)}, u32[]{:S(2)}, u32[]{:S(2)}) collective-permute-start(bf16[10,144,128]{2,1,0:T(8,128)(2,1)S(1)} %shard_map.115.refs_3_), channel_id=1, source_target_pairs={{0,1},{1,0},{2,3},{3,2},{4,5},{5,4},{6,7},{7,6},{8,9},{9,8},{10,11... | collective-permute-start | bytes 1105928 | tf_op jit(solution)/shard_map/ppermute | solution.py:436
  86.6 0.2 reshape_squeeze.3
  86.8 0.0 copy-start.6
  86.8 0.1 fusion.2
  87.0 0.4 copy.12
  87.4 0.1 copy-done.6
  87.5 3.1 %shard_map.113 = (f32[1024,512]{1,0:T(8,128)S(1)}, f32[1024,128]{1,0:T(8,128)S(1)}, f32[1024,128]{1,0:T(8,128)S(1)}) custom-call(s32[16]{0:T(128)S(1)} %copy-done.4, s32[16]{0:T(128)S(1)} %copy-done.6, bf16[1024,640]{1,0:T(8,128)(2,1)S(1)} %bitcast.48, bf16[10,144,128]{2,1,0:T(8,128)(2,1)S(1)} %shard_map.112.refs_0_), custom_call_target="tpu_custom_call" | custom-call | tf_op jit(solution)/shard_map/pallas_call | solution.py:365
  90.6 0.0 copy-start
  90.6 5.8 %shard_map.116 = (f32[1024,512]{1,0:T(8,128)S(1)}, f32[1024,128]{1,0:T(8,128)S(1)}, f32[1024,128]{1,0:T(8,128)S(1)}) custom-call(s32[16]{0:T(128)S(1)} %copy-done.4, s32[16]{0:T(128)S(1)} %copy-done.6, bf16[1024,640]{1,0:T(8,128)(2,1)S(1)} %bitcast.49, f32[1024,512]{1,0:T(8,128)S(1)} %get-tuple-element.25.refs_0_, ...), custom_call_target="tpu_custom_call" | custom-call | tf_op jit(solution)/shard_map/pallas_call | solution.py:365
  96.5 5.4 %shard_map.117 = (bf16[16,4096]{1,0:T(8,128)(2,1)S(1)}, bf16[16,4096]{1,0:T(8,128)(2,1)S(1)}) custom-call(s32[16]{0:T(128)S(1)} %copy-done.4, s32[16]{0:T(128)S(1)} %copy-done.6, bf16[1024,640]{1,0:T(8,128)(2,1)S(1)} %bitcast.50, bf16[32,512,128]{2,1,0:T(8,128)(2,1)S(1)} %copy-done, f32[1024,512]{1,0:T(8,128)S(1)} %get-tuple-element.32.acc0_ref, ...), custom_call_target="tpu_custom_call" | custom-call | tf_op jit(solution)/shard_map/pallas_call | solution.py:389
  101.9 0.6 collective-permute-start.20
  102.5 4.4 %collective-permute-done.20.refs_1_ = bf16[16,4096]{1,0:T(8,128)(2,1)S(1)} collective-permute-done((bf16[16,4096]{1,0:T(8,128)(2,1)S(1)}, bf16[16,4096]{1,0:T(8,128)(2,1)S(1)}, u32[]{:S(2)}, u32[]{:S(2)}) %collective-permute-start.20) | collective-permute-done | bytes 131104 | tf_op jit(solution)/shard_map/ppermute | solution.py:436
  106.9 0.7 shard_map.118
  (61 shorter events, 0.5 us)
Async XLA Ops:
  4.0 11.1 %collective-permute-start.9 = (f32[4,144,128]{2,1,0:T(8,128)}, f32[4,144,128]{2,1,0:T(8,128)S(1)}, u32[]{:S(2)}, u32[]{:S(2)}) collective-permute-start(f32[4,144,128]{2,1,0:T(8,128)} %bitcast.59), channel_id=1, source_target_pairs={{0,1},{1,0},{2,3},{3,2},{4,5},{5,4},{6,7},{7,6},{8,9},{9,8},{10,11... | collective-permute-start | bytes 884744 | tf_op jit(solution)/shard_map/ppermute | solution.py:436
  7.0 13.5 %collective-permute-start = (f32[4,144,128]{2,1,0:T(8,128)}, f32[4,144,128]{2,1,0:T(8,128)S(1)}, u32[]{:S(2)}, u32[]{:S(2)}) collective-permute-start(f32[4,144,128]{2,1,0:T(8,128)} %bitcast.58), channel_id=1, source_target_pairs={{0,1},{1,0},{2,3},{3,2},{4,5},{5,4},{6,7},{7,6},{8,9},{9,8},{10,11... | collective-permute-start | bytes 884744 | tf_op jit(solution)/shard_map/ppermute | solution.py:436
  7.1 8.0 %copy-start.3 = (s32[16,10]{1,0:T(8,128)S(1)}, s32[16,10]{1,0:T(8,128)}, u32[]{:S(2)}) copy-start(s32[16,10]{1,0:T(8,128)} %table_ref.7) | copy-start | bytes 1924
  7.1 8.0 %copy-start.4 = (s32[16]{0:T(128)S(1)}, s32[16]{0:T(128)}, u32[]{:S(2)}) copy-start(s32[16]{0:T(128)} %dest_ref.13) | copy-start | bytes 196
  7.1 8.0 %copy-start.5 = (f32[512]{0:T(512)S(1)}, f32[512]{0:T(512)}, u32[]{:S(2)}) copy-start(f32[512]{0:T(512)} %param.14) | copy-start | bytes 6148
  7.1 8.0 %copy-start.7 = (f32[1,128]{1,0:T(1,128)S(1)}, f32[1,128]{1,0:T(1,128)}, u32[]{:S(2)}) copy-start(f32[1,128]{1,0:T(1,128)} %constant.30.clone.freq_ref) | copy-start | bytes 1540
  15.1 1.0 copy-start.2
  17.4 5.7 %collective-permute-start.10 = (bf16[8,144,128]{2,1,0:T(8,128)(2,1)S(1)}, bf16[8,144,128]{2,1,0:T(8,128)(2,1)S(1)}, u32[]{:S(2)}, u32[]{:S(2)}) collective-permute-start(bf16[8,144,128]{2,1,0:T(8,128)(2,1)S(1)} %get-tuple-element.31), channel_id=1, source_target_pairs={{0,2},{2,0},{4,6},{6,4},{8,10},{10,8},{12,14},{14,12},{16,18},{18,... | collective-permute-start | bytes 884744 | tf_op jit(solution)/shard_map/ppermute | solution.py:441
  20.6 1.0 copy-start.1
  23.0 6.8 %collective-permute-start.1 = (bf16[8,144,128]{2,1,0:T(8,128)(2,1)S(1)}, bf16[8,144,128]{2,1,0:T(8,128)(2,1)S(1)}, u32[]{:S(2)}, u32[]{:S(2)}) collective-permute-start(bf16[8,144,128]{2,1,0:T(8,128)(2,1)S(1)} %get-tuple-element.24), channel_id=1, source_target_pairs={{0,2},{2,0},{4,6},{6,4},{8,10},{10,8},{12,14},{14,12},{16,18},{18,... | collective-permute-start | bytes 884744 | tf_op jit(solution)/shard_map/ppermute | solution.py:441
  23.2 8.2 %collective-permute-start.11 = (bf16[2,144,128]{2,1,0:T(8,128)(2,1)S(1)}, bf16[2,144,128]{2,1,0:T(8,128)(2,1)S(1)}, u32[]{:S(2)}, u32[]{:S(2)}) collective-permute-start(bf16[2,144,128]{2,1,0:T(8,128)(2,1)S(1)} %pad_maximum_fusion.7), channel_id=1, source_target_pairs={{0,4},{2,6},{4,0},{6,2},{8,12},{10,14},{12,8},{14,10},{16,20},{18,... | collective-permute-start | bytes 221192 | tf_op jit(solution)/shard_map/ppermute | solution.py:441
  25.0 10.1 %collective-permute-start.12 = (bf16[2,144,128]{2,1,0:T(8,128)(2,1)S(1)}, bf16[2,144,128]{2,1,0:T(8,128)(2,1)S(1)}, u32[]{:S(2)}, u32[]{:S(2)}) collective-permute-start(bf16[2,144,128]{2,1,0:T(8,128)(2,1)S(1)} %pad_maximum_fusion.8), channel_id=1, source_target_pairs={{0,8},{2,10},{4,12},{6,14},{8,0},{10,2},{12,4},{14,6},{16,24},{18,... | collective-permute-start | bytes 221192 | tf_op jit(solution)/shard_map/ppermute | solution.py:441
  26.7 52.1 %collective-permute-start.13 = (bf16[2,144,128]{2,1,0:T(8,128)(2,1)S(1)}, bf16[2,144,128]{2,1,0:T(8,128)(2,1)S(1)}, u32[]{:S(2)}, u32[]{:S(2)}) collective-permute-start(bf16[2,144,128]{2,1,0:T(8,128)(2,1)S(1)} %pad_maximum_fusion.9), channel_id=1, source_target_pairs={{0,12},{2,14},{4,8},{6,10},{8,4},{10,6},{12,0},{14,2},{16,28},{18,... | collective-permute-start | bytes 221192 | tf_op jit(solution)/shard_map/ppermute | solution.py:441
  26.9 53.5 %collective-permute-start.14 = (bf16[2,144,128]{2,1,0:T(8,128)(2,1)S(1)}, bf16[2,144,128]{2,1,0:T(8,128)(2,1)S(1)}, u32[]{:S(2)}, u32[]{:S(2)}) collective-permute-start(bf16[2,144,128]{2,1,0:T(8,128)(2,1)S(1)} %pad_maximum_fusion.10), channel_id=1, source_target_pairs={{0,16},{2,18},{4,20},{6,22},{8,24},{10,26},{12,28},{14,30},{16,0},... | collective-permute-start | bytes 221192 | tf_op jit(solution)/shard_map/ppermute | solution.py:441
  29.9 50.5 %collective-permute-start.15 = (bf16[2,144,128]{2,1,0:T(8,128)(2,1)S(1)}, bf16[2,144,128]{2,1,0:T(8,128)(2,1)S(1)}, u32[]{:S(2)}, u32[]{:S(2)}) collective-permute-start(bf16[2,144,128]{2,1,0:T(8,128)(2,1)S(1)} %pad_maximum_fusion.11), channel_id=1, source_target_pairs={{0,20},{2,22},{4,16},{6,18},{8,28},{10,30},{12,24},{14,26},{16,4},... | collective-permute-start | bytes 221192 | tf_op jit(solution)/shard_map/ppermute | solution.py:441
  31.4 55.2 %copy-start.9 = (bf16[1,32,2048]{2,1,0:T(8,128)(2,1)S(1)}, bf16[1,32,2048]{2,1,0:T(8,128)(2,1)}, u32[]{:S(2)}) copy-start(bf16[1,32,2048]{2,1,0:T(8,128)(2,1)} %param.16) | copy-start | bytes 393220
  31.4 49.0 %collective-permute-start.16 = (bf16[2,144,128]{2,1,0:T(8,128)(2,1)S(1)}, bf16[2,144,128]{2,1,0:T(8,128)(2,1)S(1)}, u32[]{:S(2)}, u32[]{:S(2)}) collective-permute-start(bf16[2,144,128]{2,1,0:T(8,128)(2,1)S(1)} %pad_maximum_fusion.12), channel_id=1, source_target_pairs={{0,24},{2,26},{4,28},{6,30},{8,16},{10,18},{12,20},{14,22},{16,8},... | collective-permute-start | bytes 221192 | tf_op jit(solution)/shard_map/ppermute | solution.py:441
  35.1 51.7 %copy-start.8 = (bf16[1,32,32,512]{3,2,1,0:T(8,128)(2,1)S(1)}, bf16[1,32,32,512]{3,2,1,0:T(8,128)(2,1)}, u32[]{:S(2)}) copy-start(bf16[1,32,32,512]{3,2,1,0:T(8,128)(2,1)} %param.15) | copy-start | bytes 3145732
  35.1 5.4 %collective-permute-start.2 = (bf16[2,144,128]{2,1,0:T(8,128)(2,1)S(1)}, bf16[2,144,128]{2,1,0:T(8,128)(2,1)S(1)}, u32[]{:S(2)}, u32[]{:S(2)}) collective-permute-start(bf16[2,144,128]{2,1,0:T(8,128)(2,1)S(1)} %pad_maximum_fusion), channel_id=1, source_target_pairs={{0,4},{2,6},{4,0},{6,2},{8,12},{10,14},{12,8},{14,10},{16,20},{18,... | collective-permute-start | bytes 221192 | tf_op jit(solution)/shard_map/ppermute | solution.py:441
  40.5 4.6 %collective-permute-start.3 = (bf16[2,144,128]{2,1,0:T(8,128)(2,1)S(1)}, bf16[2,144,128]{2,1,0:T(8,128)(2,1)S(1)}, u32[]{:S(2)}, u32[]{:S(2)}) collective-permute-start(bf16[2,144,128]{2,1,0:T(8,128)(2,1)S(1)} %pad_maximum_fusion.1), channel_id=1, source_target_pairs={{0,8},{2,10},{4,12},{6,14},{8,0},{10,2},{12,4},{14,6},{16,24},{18,... | collective-permute-start | bytes 221192 | tf_op jit(solution)/shard_map/ppermute | solution.py:441
  45.1 6.0 %collective-permute-start.4 = (bf16[2,144,128]{2,1,0:T(8,128)(2,1)S(1)}, bf16[2,144,128]{2,1,0:T(8,128)(2,1)S(1)}, u32[]{:S(2)}, u32[]{:S(2)}) collective-permute-start(bf16[2,144,128]{2,1,0:T(8,128)(2,1)S(1)} %pad_maximum_fusion.2), channel_id=1, source_target_pairs={{0,12},{2,14},{4,8},{6,10},{8,4},{10,6},{12,0},{14,2},{16,28},{18,... | collective-permute-start | bytes 221192 | tf_op jit(solution)/shard_map/ppermute | solution.py:441
  51.1 5.3 %collective-permute-start.5 = (bf16[2,144,128]{2,1,0:T(8,128)(2,1)S(1)}, bf16[2,144,128]{2,1,0:T(8,128)(2,1)S(1)}, u32[]{:S(2)}, u32[]{:S(2)}) collective-permute-start(bf16[2,144,128]{2,1,0:T(8,128)(2,1)S(1)} %pad_maximum_fusion.3), channel_id=1, source_target_pairs={{0,16},{2,18},{4,20},{6,22},{8,24},{10,26},{12,28},{14,30},{16,0},... | collective-permute-start | bytes 221192 | tf_op jit(solution)/shard_map/ppermute | solution.py:441
  56.4 7.4 %collective-permute-start.6 = (bf16[2,144,128]{2,1,0:T(8,128)(2,1)S(1)}, bf16[2,144,128]{2,1,0:T(8,128)(2,1)S(1)}, u32[]{:S(2)}, u32[]{:S(2)}) collective-permute-start(bf16[2,144,128]{2,1,0:T(8,128)(2,1)S(1)} %pad_maximum_fusion.4), channel_id=1, source_target_pairs={{0,20},{2,22},{4,16},{6,18},{8,28},{10,30},{12,24},{14,26},{16,4},... | collective-permute-start | bytes 221192 | tf_op jit(solution)/shard_map/ppermute | solution.py:441
  63.8 6.2 %collective-permute-start.7 = (bf16[2,144,128]{2,1,0:T(8,128)(2,1)S(1)}, bf16[2,144,128]{2,1,0:T(8,128)(2,1)S(1)}, u32[]{:S(2)}, u32[]{:S(2)}) collective-permute-start(bf16[2,144,128]{2,1,0:T(8,128)(2,1)S(1)} %pad_maximum_fusion.5), channel_id=1, source_target_pairs={{0,24},{2,26},{4,28},{6,30},{8,16},{10,18},{12,20},{14,22},{16,8},... | collective-permute-start | bytes 221192 | tf_op jit(solution)/shard_map/ppermute | solution.py:441
  70.0 7.0 %collective-permute-start.8 = (bf16[2,144,128]{2,1,0:T(8,128)(2,1)S(1)}, bf16[2,144,128]{2,1,0:T(8,128)(2,1)S(1)}, u32[]{:S(2)}, u32[]{:S(2)}) collective-permute-start(bf16[2,144,128]{2,1,0:T(8,128)(2,1)S(1)} %pad_maximum_fusion.6), channel_id=1, source_target_pairs={{0,28},{2,30},{4,24},{6,26},{8,20},{10,22},{12,16},{14,18},{16,12}... | collective-permute-start | bytes 221192 | tf_op jit(solution)/shard_map/ppermute | solution.py:441
  77.0 7.0 %collective-permute-start.17 = (bf16[2,144,128]{2,1,0:T(8,128)(2,1)S(1)}, bf16[2,144,128]{2,1,0:T(8,128)(2,1)S(1)}, u32[]{:S(2)}, u32[]{:S(2)}) collective-permute-start(bf16[2,144,128]{2,1,0:T(8,128)(2,1)S(1)} %pad_maximum_fusion.13), channel_id=1, source_target_pairs={{0,28},{2,30},{4,24},{6,26},{8,20},{10,22},{12,16},{14,18},{16,12}... | collective-permute-start | bytes 221192 | tf_op jit(solution)/shard_map/ppermute | solution.py:441
  78.8 11.8 %collective-permute-start.18 = (bf16[10,144,128]{2,1,0:T(8,128)(2,1)S(1)}, bf16[10,144,128]{2,1,0:T(8,128)(2,1)S(1)}, u32[]{:S(2)}, u32[]{:S(2)}) collective-permute-start(bf16[10,144,128]{2,1,0:T(8,128)(2,1)S(1)} %shard_map.112.refs_0_), channel_id=1, source_target_pairs={{0,1},{1,0},{2,3},{3,2},{4,5},{5,4},{6,7},{7,6},{8,9},{9,8},{10,11... | collective-permute-start | bytes 1105928 | tf_op jit(solution)/shard_map/ppermute | solution.py:436
  85.0 11.4 %collective-permute-start.19 = (bf16[10,144,128]{2,1,0:T(8,128)(2,1)S(1)}, bf16[10,144,128]{2,1,0:T(8,128)(2,1)S(1)}, u32[]{:S(2)}, u32[]{:S(2)}) collective-permute-start(bf16[10,144,128]{2,1,0:T(8,128)(2,1)S(1)} %shard_map.115.refs_3_), channel_id=1, source_target_pairs={{0,1},{1,0},{2,3},{3,2},{4,5},{5,4},{6,7},{7,6},{8,9},{9,8},{10,11... | collective-permute-start | bytes 1105928 | tf_op jit(solution)/shard_map/ppermute | solution.py:436
  86.8 0.7 copy-start.6
  90.6 5.9 %copy-start = (bf16[32,512,128]{2,1,0:T(8,128)(2,1)S(1)}, bf16[32,512,128]{2,1,0:T(8,128)(2,1)}, u32[]{:S(2)}) copy-start(bf16[32,512,128]{2,1,0:T(8,128)(2,1)} %w_ref.1) | copy-start | bytes 12582916
  101.9 5.0 %collective-permute-start.20 = (bf16[16,4096]{1,0:T(8,128)(2,1)S(1)}, bf16[16,4096]{1,0:T(8,128)(2,1)S(1)}, u32[]{:S(2)}, u32[]{:S(2)}) collective-permute-start(bf16[16,4096]{1,0:T(8,128)(2,1)S(1)} %get-tuple-element.36), channel_id=1, source_target_pairs={{0,1},{1,0},{2,3},{3,2},{4,5},{5,4},{6,7},{7,6},{8,9},{9,8},{10,11... | collective-permute-start | bytes 393224 | tf_op jit(solution)/shard_map/ppermute | solution.py:436

commit v2 on v1

--- a/solution.py
+++ b/solution.py
@@ -21,6 +21,7 @@
 
 MIB = 1024 * 1024
 PART_MIB, END_MIB = 24, 24
+CUTS = 2
 
 
 def params(mib):
@@ -31,13 +32,11 @@
     return lax.dot_general(a, b, (((1,), (1,)), ((), ())), preferred_element_type=F32)
 
 
-def project_kernel(
-    share_ref, hid_ref, wl_ref, wr_ref, *refs, chunks, pages, tokens, parts, shares
-):
-    outs, (hid_buf, wl_buf, wr_buf, sems) = refs[:chunks], refs[chunks:]
-    share = tokens * chunks
-    half = tokens // 2
-    depth = hid_ref.shape[-1] // parts
+def project_kernel(share_ref, hid_ref, wl_ref, wr_ref, *refs, which, parts):
+    count = len(which)
+    outs, (hid_buf, wl_buf, wr_buf, sems) = refs[:count], refs[count:]
+    pages, _, _, tokens, features = hid_ref.shape
+    half, depth = tokens // 2, features // parts
     copies = []
     for k in range(parts):
         at = pl.ds(k * depth, depth)
@@ -48,65 +47,64 @@
             ]
             + [
                 pltpu.make_async_copy(
-                    hid_ref.at[:, share_ref[s], :, at], hid_buf.at[s, :, :, at], sems.at[2 + s, k]
+                    hid_ref.at[:, share_ref[n], chunk, :, at], hid_buf.at[n, :, :, at], sems.at[2 + n, k]
                 )
-                for s in range(shares)
+                for n, chunk in enumerate(which)
             ]
         )
     for group in copies:
         for copy in group:
             copy.start()
-    for s in range(shares):
-        lat = rope = None
-        for k in range(parts):
-            for copy in copies[k] if s == 0 else ():
-                copy.wait()
-            rows = hid_buf[s, :, :, k * depth : (k + 1) * depth].reshape(pages * share, depth)
-            wide = jnp.dot(rows, wl_buf[k * depth : (k + 1) * depth], preferred_element_type=F32)
-            side = nt_dot(rows, wr_buf[:, k * depth : (k + 1) * depth])
-            lat, rope = (wide, side) if k == 0 else (lat + wide, rope + side)
-        blocks = lat.shape[1] // LANES
+    lat = rope = None
+    for k in range(parts):
+        for copy in copies[k]:
+            copy.wait()
+        rows = hid_buf[:, :, :, k * depth : (k + 1) * depth].reshape(count * pages * tokens, depth)
+        wide = jnp.dot(rows, wl_buf[k * depth : (k + 1) * depth], preferred_element_type=F32)
+        side = nt_dot(rows, wr_buf[:, k * depth : (k + 1) * depth])
+        lat, rope = (wide, side) if k == 0 else (lat + wide, rope + side)
+    blocks = lat.shape[1] // LANES
+    for n in range(count):
         for page in range(pages):
-            for c in range(chunks):
-                at = (page * chunks + c) * tokens
-                for b in range(blocks):
-                    outs[c][s, page, b * tokens : (b + 1) * tokens] = lat[
-                        at : at + tokens, b * LANES : (b + 1) * LANES
-                    ]
-                outs[c][s, page, blocks * tokens :] = jnp.concatenate(
-                    [rope[at : at + half], rope[at + half : at + tokens]], axis=1
-                )
-
-
-def project(hidden, w_latent, w_rope, shares, head_count, chunks, keep=False):
+            at = (n * pages + page) * tokens
+            for b in range(blocks):
+                outs[n][page, b * tokens : (b + 1) * tokens] = lat[
+                    at : at + tokens, b * LANES : (b + 1) * LANES
+                ]
+            outs[n][page, blocks * tokens :] = jnp.concatenate(
+                [rope[at : at + half], rope[at + half : at + tokens]], axis=1
+            )
+
+
+def project(hidden, w_latent, w_rope, wanted, planes, chunks, mib):
     features = hidden.shape[1]
     pages = hidden.shape[0] // PAGE
-    share = PAGE // head_count
-    tokens = share // chunks
+    tokens = PAGE // planes // chunks
     parts = next(n for n in (5, 4, 2, 1) if features % (n * LANES) == 0)
     rows = tokens * (w_latent.shape[1] // LANES) + tokens // 2
-    count = shares.shape[0]
-    view = hidden.reshape(pages, head_count, share, features)
+    count = len(wanted)
+    view = hidden.reshape(pages, planes, chunks, tokens, features)
+    shares = sum(
+        jnp.where(jnp.arange(count) == n, share, 0) for n, (share, _) in enumerate(wanted)
+    ).astype(jnp.int32)
     side = w_rope.T
-    hbm = pl.BlockSpec(memory_space=pltpu.HBM)
-    flops = 2 * count * pages * share * features * (w_latent.shape[1] + w_rope.shape[1])
+    hbm = pl.BlockSpec(memory_space=pl.ANY)
+    flops = 2 * count * pages * tokens * features * (w_latent.shape[1] + w_rope.shape[1])
     return pl.pallas_call(
-        functools.partial(
-            project_kernel, chunks=chunks, pages=pages, tokens=tokens, parts=parts, shares=count
-        ),
+        functools.partial(project_kernel, which=tuple(c for _, c in wanted), parts=parts),
         in_specs=[pl.BlockSpec(memory_space=pltpu.SMEM), hbm, hbm, hbm],
-        out_specs=[pl.BlockSpec(memory_space=pltpu.VMEM)] * chunks,
-        out_shape=[jax.ShapeDtypeStruct((count, pages, rows, LANES), F32)] * chunks,
+        out_specs=[pl.BlockSpec(memory_space=pltpu.VMEM)] * count,
+        out_shape=[jax.ShapeDtypeStruct((pages, rows, LANES), F32)] * count,
         scratch_shapes=[
-            pltpu.VMEM((count, pages, share, features), BF16),
+            pltpu.VMEM((count, pages, tokens, features), BF16),
             pltpu.VMEM(w_latent.shape, BF16),
             pltpu.VMEM(side.shape, BF16),
             pltpu.SemaphoreType.DMA((2 + count, parts)),
         ],
-        compiler_params=params(63 if count > 1 or not keep else 62),
+        compiler_params=params(mib),
         cost_estimate=pl.CostEstimate(
             flops=flops,
-            bytes_accessed=2 * features * (count * pages * share + w_latent.shape[1] + LANES),
+            bytes_accessed=2 * features * (count * pages * tokens + w_latent.shape[1] + LANES),
             transcendentals=0,
         ),
     )(shares, view, w_latent, side)
@@ -122,7 +120,7 @@
 def finish_kernel(dest_ref, table_ref, gain_ref, freq_ref, own_ref, *refs, tokens, blocks, chunk, share):
     terms, outs, page_ref = refs[:-3], refs[-3:-1], refs[-1]
     me, head = lax.axis_index("tok"), lax.axis_index("head")
-    pages = own_ref.shape[1]
+    pages = own_ref.shape[0]
     half = tokens // 2
     table = table_ref[...]
     request = lax.broadcasted_iota(jnp.int32, table.shape, 0)
@@ -131,13 +129,13 @@
     row = lax.broadcasted_iota(jnp.int32, (half, LANES), 0)
     low = (lane % 64) < 32
     inside = row + (lane // 64) * half + (head * share + chunk * tokens)
+    hits = [table == me * pages + page for page in range(pages)]
+    slots = [jnp.sum(jnp.where(hit, listed, 0)) for hit in hits]
+    owners = [jnp.sum(jnp.where(hit, request, 0)) for hit in hits]
     for page in range(pages):
-        hit = table == me * pages + page
-        slot = jnp.sum(jnp.where(hit, listed, 0))
-        group = dest_ref[jnp.sum(jnp.where(hit, request, 0))]
 
         def total(lo, hi, page=page):
-            value = own_ref[0, page, lo:hi]
+            value = own_ref[page, lo:hi]
             for term in terms:
                 value = value + term[page, lo:hi]
             return value
@@ -151,10 +149,12 @@
         scaled = [(part * inverse * gain_ref[b : b + 1]).astype(BF16) for b, part in enumerate(parts)]
         raw = total(blocks * tokens, blocks * tokens + half).astype(BF16).astype(F32)
         other = jnp.where(low, -pltpu.roll(raw, LANES - 32, 1), pltpu.roll(raw, 32, 1))
-        angle = freq_ref[...] * (inside + slot * PAGE).astype(F32)
+        angle = freq_ref[...] * (inside + slots[page] * PAGE).astype(F32)
         turned = raw * jnp.cos(angle) + other * jnp.sin(angle)
         page_ref[page, : blocks * tokens] = jnp.concatenate(scaled, axis=0)
         page_ref[page, blocks * tokens :] = turned.astype(BF16)
+    for page in range(pages):
+        group = dest_ref[owners[page]]
         place = lax.bitwise_xor(group // 2, me // 2)
         same = group % 2 == me % 2
 
@@ -168,7 +168,7 @@
 
 
 def finish(dest, table, gain, freq, own, terms, tokens, chunk, share):
-    _, pages, rows, _ = own.shape
+    pages, rows, _ = own.shape
     blocks = gain.shape[0]
     vmem = pl.BlockSpec(memory_space=pltpu.VMEM)
     half_groups = max(dest.shape[0] // 2, 1)
@@ -182,7 +182,8 @@
     )(dest, table, gain, freq, own, *terms)
 
 
-def select_kernel(dest_ref, table_ref, in_ref, out_ref, *, pages):
+def select_kernel(dest_ref, table_ref, *refs, pages):
+    ins, out_ref = refs[:-1], refs[-1]
     me = lax.axis_index("tok")
     request = request_of(dest_ref, me)
     first = table_ref[request, 0]
@@ -190,18 +191,29 @@
         listed = table_ref[request, slot]
         source = lax.div(jnp.where(listed >= 0, listed, first), pages)
         place = lax.bitwise_xor(lax.div(source, 2), lax.div(me, 2))
-        out_ref[slot] = in_ref[place, lax.rem(source + me, 2)]
-
-
-def select(dest, table, arrived, pages):
+        if len(ins) == 1:
+            out_ref[slot] = ins[0][place, lax.rem(source + me, 2)]
+            continue
+        same = lax.rem(source + me, 2) == 0
+
+        @pl.when(same)
+        def _(slot=slot, place=place):
+            out_ref[slot] = ins[0][place]
+
+        @pl.when(jnp.logical_not(same))
+        def _(slot=slot, place=place):
+            out_ref[slot] = ins[1][place]
+
+
+def select(dest, table, landed, pages):
     vmem, smem = pl.BlockSpec(memory_space=pltpu.VMEM), pl.BlockSpec(memory_space=pltpu.SMEM)
     return pl.pallas_call(
         functools.partial(select_kernel, pages=pages),
-        in_specs=[smem, smem, vmem],
+        in_specs=[smem, smem] + [vmem] * len(landed),
         out_specs=vmem,
-        out_shape=jax.ShapeDtypeStruct((table.shape[1],) + arrived.shape[2:], BF16),
+        out_shape=jax.ShapeDtypeStruct((table.shape[1],) + landed[0].shape[-2:], BF16),
         compiler_params=params(8),
-    )(dest, table, arrived)
+    )(dest, table, *landed)
 
 
 def fold(value, op):
@@ -316,37 +328,51 @@
 
 
 def end_kernel(
-    dest_ref, len_ref, q_ref, w_ref, acc0_ref, top0_ref, sum0_ref, *refs,
-    origins, planes, chunks, tokens, width, rows_q,
+    dest_ref, len_ref, q_ref, w_ref, acc_ref, top_ref, sum_ref, *refs,
+    origins, planes, chunks, tokens, width, rows_q, cuts,
 ):
     payloads = refs[: len(origins)]
     outs = refs[len(origins) : len(origins) + planes]
-    key_ref, score_ref, acc_ref, top_ref, sum_ref, map_ref, w_buf, w_sem = refs[len(origins) + planes :]
+    key_ref, score_ref, map_ref, w_buf, w_sem = refs[len(origins) + planes :]
     w_copy = pltpu.make_async_copy(w_ref, w_buf, w_sem)
     w_copy.start()
     head = lax.axis_index("head")
     context = len_ref[request_of(dest_ref, lax.axis_index("tok"))]
     offsets = payload_offsets(origins, planes, chunks, tokens)
-    slots = payloads[0].shape[0]
-    count = q_ref.shape[0]
     fill_keys(key_ref, payloads, tokens, width)
-    top = start_state(
-        acc_ref, top_ref, sum_ref, (acc0_ref, top0_ref, sum0_ref),
-        lambda: score_keys(
-            q_ref, key_ref, score_ref, top_ref,
-            lambda at, step: dead_bias(at, step, context, slots, tokens, offsets),
-        ),
-    )
-    weigh_keys(key_ref, score_ref, acc_ref, sum_ref, top, width)
+    blocks, _, step = score_ref.shape
     owned = rows_q // planes
-    inverse = 1.0 / jnp.sum(sum_ref[...], axis=1, keepdims=True)
-    w_copy.wait()
-    for h in range(count // rows_q):
-        rows = slice(h * rows_q, (h + 1) * rows_q)
-        attended = (acc_ref[rows] * inverse[rows]).astype(BF16)
-        mapped = jnp.dot(attended, w_buf[h], preferred_element_type=F32)
-        for p in range(planes):
-            map_ref[p, :, h * LANES : (h + 1) * LANES] = mapped[p * owned : (p + 1) * owned]
+    part = q_ref.shape[0] // cuts
+    biases = [
+        dead_bias(i * step, step, context, payloads[0].shape[0], tokens, offsets) for i in range(blocks)
+    ]
+    for cut in range(cuts):
+        rows = slice(cut * part, (cut + 1) * part)
+        scores = [
+            nt_dot(q_ref[rows], key_ref[i * step : (i + 1) * step]) + biases[i] for i in range(blocks)
+        ]
+        peak = functools.reduce(jnp.maximum, [fold(x, jnp.maximum) for x in scores])
+        before = top_ref[rows]
+        top = jnp.maximum(jnp.max(peak, axis=1, keepdims=True), before[:, :1])
+        factor = jnp.exp2((before[:, :1] - top) * (SCALE * LOG2E))
+        weights = [jnp.exp2((x - top) * (SCALE * LOG2E)) for x in scores]
+        total = functools.reduce(jnp.add, [fold(x, jnp.add) for x in weights]) + sum_ref[rows] * factor
+        inverse = 1.0 / jnp.sum(total, axis=1, keepdims=True)
+        summed = acc_ref[rows] * factor
+        for i, x in enumerate(weights):
+            summed += jnp.dot(
+                x.astype(BF16), key_ref[i * step : (i + 1) * step, :width], preferred_element_type=F32
+            )
+        attended = (summed * inverse).astype(BF16)
+        if cut == 0:
+            w_copy.wait()
+        for h in range(part // rows_q):
+            at = cut * (part // rows_q) + h
+            mapped = jnp.dot(
+                attended[h * rows_q : (h + 1) * rows_q], w_buf[at], preferred_element_type=F32
+            )
+            for p in range(planes):
+                map_ref[p, :, at * LANES : (at + 1) * LANES] = mapped[p * owned : (p + 1) * owned]
     for d in range(planes):
         outs[d][...] = map_ref[lax.rem(head + d, planes)].astype(BF16)
 
@@ -385,7 +411,6 @@
     count = query.shape[0]
     rows_q = count // heads
     vmem, smem = pl.BlockSpec(memory_space=pltpu.VMEM), pl.BlockSpec(memory_space=pltpu.SMEM)
-    state = [(count, lat), (count, LANES), (count, LANES)]
     return pl.pallas_call(
         functools.partial(
             end_kernel,
@@ -395,12 +420,12 @@
             tokens=tokens,
             width=lat,
             rows_q=rows_q,
+            cuts=CUTS if heads % CUTS == 0 else 1,
         ),
         in_specs=[smem, smem, vmem, pl.BlockSpec(memory_space=pltpu.HBM)] + [vmem] * (3 + len(payloads)),
         out_specs=[vmem] * planes,
         out_shape=[jax.ShapeDtypeStruct((rows_q // planes, heads * LANES), BF16)] * planes,
         scratch_shapes=key_scratch(list(payloads.values()), tokens, count, lat)
-        + [pltpu.VMEM(shape, F32) for shape in state]
         + [
             pltpu.VMEM((planes, rows_q // planes, heads * LANES), F32),
             pltpu.VMEM(w_value.shape, BF16),
@@ -456,12 +481,16 @@
     blocks = w_latent.shape[1] // LANES
     rope_width = w_rope.shape[1]
 
-    others = (my_head + 1 + jnp.arange(planes - 1, dtype=jnp.int32)) % planes
-    sent = project(hidden, w_latent, w_rope, others.astype(jnp.int32), planes, chunks)
+    others = [(my_head + d) % planes for d in range(1, planes)]
+    sent = project(hidden, w_latent, w_rope, [(o, 0) for o in others], planes, chunks, 63)
+    rest = [(o, c) for c in range(1, chunks) for o in others] + [(my_head, c) for c in range(chunks)]
+    rest = project(hidden, w_latent, w_rope, rest, planes, chunks, 58)
+    sent, own = list(sent) + list(rest[:-chunks]), rest[-chunks:]
     arrived = []
     for c in range(chunks):
-        arrived.append([shift(sent[c][d - 1], "head", d) for d in range(1, planes)])
-    own = project(hidden, w_latent, w_rope, my_head[None].astype(jnp.int32), planes, chunks, True)
+        arrived.append(
+            [shift(sent[c * (planes - 1) + d - 1], "head", d) for d in range(1, planes)]
+        )
 
     rows_q, heads = q_latent.shape[1], q_latent.shape[2]
     query_side = q_rope[0].reshape(rows_q, heads, rope_width)
@@ -479,11 +508,18 @@
         mine, other = finish(
             dest_group, page_table, gain, freq, own[c], arrived[c], tokens, c, share
         )
-        got = trade(other, 1)
-        landed = [jnp.stack([mine[0], got[0]])]
+        late = c == 0
+        if not late:
+            other = trade(other, 1)
+        landed = [jnp.stack([mine[0], other[0]])]
         for k in range(1, groups // 2):
-            landed.append(trade(jnp.stack([mine[k], got[k]]), 2 * k))
-        picked.append(select(dest_group, page_table, jnp.stack(landed), pages))
+            landed.append(trade(jnp.stack([mine[k], other[k]]), 2 * k))
+        if late:
+            crossed = trade(jnp.stack([x[1] for x in landed]), 1)
+            landed = [jnp.stack([x[0] for x in landed]), crossed]
+        else:
+            landed = [jnp.stack(landed)]
+        picked.append(select(dest_group, page_table, landed, pages))
     sent_keys = []
     for c in range(chunks):
         sent_keys.append({(d, c): shift(picked[c], "head", d) for d in range(1, planes)})
@@ -514,6 +550,4 @@
         P(),
         P(),
     )
-    return jax.shard_map(
-        run_device, mesh=mesh, in_specs=placed, out_specs=P("tok", "head", None), check_vma=False
-    )
+    return jax.shard_map(run_device, mesh=mesh, in_specs=placed, out_specs=P("tok", "head", None), check_vma=False)

time: 108 us -> 93.2 us (0.86)
  waiting for transfers between devices: 54.2 us -> 26.3 us
  starting transfers between devices: 22 us -> 36.7 us
  local copies, waits for them, and re-layouts: 3 us -> 1.09 us
    ppermute x16, waiting for transfers between devices: 42.8 us -> 13.6 us  [trade(): return lax.ppermute(value, 'tok', [(i, i ^ mask) for i in range(count)])]
    ppermute x16, starting transfers between devices: 15.2 us -> 29 us  [trade(): return lax.ppermute(value, 'tok', [(i, i ^ mask) for i in range(count)])]
    unnamed x32 -> x33, local copies, waits for them, and re-layouts: 2.22 us -> 0.37 us
    ppermute x5, waiting for transfers between devices: 11.5 us -> 12.7 us  [shift(): lax.ppermute(value, axis, [(i, (i + by) % count) for i in range(count)])]
  transfers between devices with their start and end apart: 21 -> 21, of which waited for: 11 -> 8; matrix products, arithmetic and copies ran while one was open for 1% -> 1% of each run, Pallas kernels for 16% -> 17%
where the time goes in v2:
time: 93.2 us; the launch traced here: 92.8 us
  starting transfers between devices  36.7 us (39%)
  Pallas kernels  27.4 us (29%)
  waiting for transfers between devices  26.3 us (28%)
  local copies, waits for them, and re-layouts  1.09 us (1%)
    ppermute x16, starting transfers between devices, trade(): return lax.ppermute(value, 'tok', [(i, i ^ mask) for i in range(count)])  29 us
    ppermute x16, waiting for transfers between devices, trade(): return lax.ppermute(value, 'tok', [(i, i ^ mask) for i in range(count)])  13.6 us
    ppermute x5, waiting for transfers between devices, shift(): lax.ppermute(value, axis, [(i, (i + by) % count) for i in range(count)])  12.7 us
    pallas_call x2, Pallas kernels, attend_part(): pl.pallas_call(functools.partial(part_kernel, carry=len(carried), origins...  8.98 us
    pallas_call x2, Pallas kernels, project(): pl.pallas_call(functools.partial(project_kernel, which=tuple((c for _, c...  8.8 us
    ppermute x5, starting transfers between devices, shift(): lax.ppermute(value, axis, [(i, (i + by) % count) for i in range(count)])  7.68 us
    pallas_call x1, Pallas kernels, attend_end(): pl.pallas_call(functools.partial(end_kernel, origins=tuple(payloads), pla...  5.14 us
    pallas_call x2, Pallas kernels, select(): pl.pallas_call(functools.partial(select_kernel, pages=pages), in_specs=[s...  2 us
  transfers between devices with their start and end apart: 21, of which 8 were waited for; matrix products, arithmetic and copies ran while one was open for 1% of the time, Pallas kernels for 17%

profile of v2, /device:TPU:0, one launch (start us, length us, event | category | flops | bytes accessed | tf_op | source)
XLA Modules:
  0.0 92.8 jit_solution(6148416082251923892)
XLA Ops:
  0.0 0.6 fusion.5.share_ref
  0.6 5.5 %shard_map.109 = (f32[4,144,128]{2,1,0:T(8,128)}, f32[4,144,128]{2,1,0:T(8,128)}, f32[4,144,128]{2,1,0:T(8,128)}) custom-call(s32[3]{0:T(128)} %fusion.5.share_ref, bf16[4,2,2,32,2560]{4,3,2,1,0:T(8,128)(2,1)} %bitcast.32, bf16[2560,512]{1,0:T(8,128)(2,1)} %wl_ref.3, bf16[64,2560]{1,0:T(8,128)(2,1)} %bitcast.34), custom_call_target="tpu_custom_call" | custom-call | flops 1132462080 | bytes 5242880 | tf_op jit(solution)/shard_map/pallas_call | solution.py:93
  6.1 3.0 %collective-permute-start.9 = (f32[4,144,128]{2,1,0:T(8,128)}, f32[4,144,128]{2,1,0:T(8,128)S(1)}, u32[]{:S(2)}, u32[]{:S(2)}) collective-permute-start(f32[4,144,128]{2,1,0:T(8,128)} %get-tuple-element.27), channel_id=1, source_target_pairs={{0,1},{1,0},{2,3},{3,2},{4,5},{5,4},{6,7},{7,6},{8,9},{9,8},{10,11... | collective-permute-start | bytes 884744 | tf_op jit(solution)/shard_map/ppermute | solution.py:461
  9.2 0.0 copy-start.7
  9.2 3.3 %shard_map.110 = f32[4,144,128]{2,1,0:T(8,128)} custom-call(s32[1]{0:T(128)} %bitcast.6.share_ref, bf16[4,2,2,32,2560]{4,3,2,1,0:T(8,128)(2,1)} %bitcast.33, bf16[2560,512]{1,0:T(8,128)(2,1)} %wl_ref.3, bf16[64,2560]{1,0:T(8,128)(2,1)} %bitcast.35), custom_call_target="tpu_custom_call" | custom-call | flops 377487360 | bytes 3932160 | tf_op jit(solution)/shard_map/pallas_call | solution.py:93
  12.5 0.2 collective-permute-start
  12.6 4.6 %collective-permute-done.9.refs_0_ = f32[4,144,128]{2,1,0:T(8,128)S(1)} collective-permute-done((f32[4,144,128]{2,1,0:T(8,128)}, f32[4,144,128]{2,1,0:T(8,128)S(1)}, u32[]{:S(2)}, u32[]{:S(2)}) %collective-permute-start.9) | collective-permute-done | bytes 294944 | tf_op jit(solution)/shard_map/ppermute | solution.py:461
  17.3 0.9 shard_map.114
  18.2 0.1 collective-permute-start.10
  18.3 4.4 %collective-permute-done.refs_0_ = f32[4,144,128]{2,1,0:T(8,128)S(1)} collective-permute-done((f32[4,144,128]{2,1,0:T(8,128)}, f32[4,144,128]{2,1,0:T(8,128)S(1)}, u32[]{:S(2)}, u32[]{:S(2)}) %collective-permute-start) | collective-permute-done | bytes 294944 | tf_op jit(solution)/shard_map/ppermute | solution.py:461
  22.7 0.9 shard_map.111
  23.7 4.9 %collective-permute-start.7 = (bf16[2,144,128]{2,1,0:T(8,128)(2,1)S(1)}, bf16[2,144,128]{2,1,0:T(8,128)(2,1)S(1)}, u32[]{:S(2)}, u32[]{:S(2)}) collective-permute-start(bf16[2,144,128]{2,1,0:T(8,128)(2,1)S(1)} %pad_maximum_fusion.6), channel_id=1, source_target_pairs={{0,28},{2,30},{4,24},{6,26},{8,20},{10,22},{12,16},{14,18},{16,12}... | collective-permute-start | bytes 221192 | tf_op jit(solution)/shard_map/ppermute | solution.py:466
  28.6 0.3 collective-permute-start.6
  28.9 0.8 collective-permute-start.5
  29.7 1.6 %collective-permute-start.1 = (bf16[2,144,128]{2,1,0:T(8,128)(2,1)S(1)}, bf16[2,144,128]{2,1,0:T(8,128)(2,1)S(1)}, u32[]{:S(2)}, u32[]{:S(2)}) collective-permute-start(bf16[2,144,128]{2,1,0:T(8,128)(2,1)S(1)} %pad_maximum_fusion), channel_id=1, source_target_pairs={{0,4},{2,6},{4,0},{6,2},{8,12},{10,14},{12,8},{14,10},{16,20},{18,... | collective-permute-start | bytes 221192 | tf_op jit(solution)/shard_map/ppermute | solution.py:466
  31.3 3.1 %collective-permute-done.1 = bf16[2,144,128]{2,1,0:T(8,128)(2,1)S(1)} collective-permute-done((bf16[2,144,128]{2,1,0:T(8,128)(2,1)S(1)}, bf16[2,144,128]{2,1,0:T(8,128)(2,1)S(1)}, u32[]{:S(2)}, u32[]{:S(2)}) %collective-permute-start.1) | collective-permute-done | bytes 73760 | tf_op jit(solution)/shard_map/ppermute | solution.py:466
  34.5 3.0 %collective-permute-start.2 = (bf16[2,144,128]{2,1,0:T(8,128)(2,1)S(1)}, bf16[2,144,128]{2,1,0:T(8,128)(2,1)S(1)}, u32[]{:S(2)}, u32[]{:S(2)}) collective-permute-start(bf16[2,144,128]{2,1,0:T(8,128)(2,1)S(1)} %pad_maximum_fusion.1), channel_id=1, source_target_pairs={{0,8},{2,10},{4,12},{6,14},{8,0},{10,2},{12,4},{14,6},{16,24},{18,... | collective-permute-start | bytes 221192 | tf_op jit(solution)/shard_map/ppermute | solution.py:466
  37.5 2.3 %collective-permute-done.2 = bf16[2,144,128]{2,1,0:T(8,128)(2,1)S(1)} collective-permute-done((bf16[2,144,128]{2,1,0:T(8,128)(2,1)S(1)}, bf16[2,144,128]{2,1,0:T(8,128)(2,1)S(1)}, u32[]{:S(2)}, u32[]{:S(2)}) %collective-permute-start.2) | collective-permute-done | bytes 73760 | tf_op jit(solution)/shard_map/ppermute | solution.py:466
  39.8 3.3 %collective-permute-start.3 = (bf16[2,144,128]{2,1,0:T(8,128)(2,1)S(1)}, bf16[2,144,128]{2,1,0:T(8,128)(2,1)S(1)}, u32[]{:S(2)}, u32[]{:S(2)}) collective-permute-start(bf16[2,144,128]{2,1,0:T(8,128)(2,1)S(1)} %pad_maximum_fusion.2), channel_id=1, source_target_pairs={{0,12},{2,14},{4,8},{6,10},{8,4},{10,6},{12,0},{14,2},{16,28},{18,... | collective-permute-start | bytes 221192 | tf_op jit(solution)/shard_map/ppermute | solution.py:466
  43.1 2.3 %collective-permute-done.3 = bf16[2,144,128]{2,1,0:T(8,128)(2,1)S(1)} collective-permute-done((bf16[2,144,128]{2,1,0:T(8,128)(2,1)S(1)}, bf16[2,144,128]{2,1,0:T(8,128)(2,1)S(1)}, u32[]{:S(2)}, u32[]{:S(2)}) %collective-permute-start.3) | collective-permute-done | bytes 73760 | tf_op jit(solution)/shard_map/ppermute | solution.py:466
  45.4 2.8 %collective-permute-start.4 = (bf16[2,144,128]{2,1,0:T(8,128)(2,1)S(1)}, bf16[2,144,128]{2,1,0:T(8,128)(2,1)S(1)}, u32[]{:S(2)}, u32[]{:S(2)}) collective-permute-start(bf16[2,144,128]{2,1,0:T(8,128)(2,1)S(1)} %pad_maximum_fusion.3), channel_id=1, source_target_pairs={{0,16},{2,18},{4,20},{6,22},{8,24},{10,26},{12,28},{14,30},{16,0},... | collective-permute-start | bytes 221192 | tf_op jit(solution)/shard_map/ppermute | solution.py:466
  48.2 2.5 %collective-permute-done.4 = bf16[2,144,128]{2,1,0:T(8,128)(2,1)S(1)} collective-permute-done((bf16[2,144,128]{2,1,0:T(8,128)(2,1)S(1)}, bf16[2,144,128]{2,1,0:T(8,128)(2,1)S(1)}, u32[]{:S(2)}, u32[]{:S(2)}) %collective-permute-start.4) | collective-permute-done | bytes 73760 | tf_op jit(solution)/shard_map/ppermute | solution.py:466
  50.8 0.1 collective-permute-start.8
  50.9 0.0 copy-start.9
  50.9 1.9 %collective-permute-start.11 = (bf16[2,144,128]{2,1,0:T(8,128)(2,1)S(1)}, bf16[2,144,128]{2,1,0:T(8,128)(2,1)S(1)}, u32[]{:S(2)}, u32[]{:S(2)}) collective-permute-start(bf16[2,144,128]{2,1,0:T(8,128)(2,1)S(1)} %pad_maximum_fusion.7), channel_id=1, source_target_pairs={{0,4},{2,6},{4,0},{6,2},{8,12},{10,14},{12,8},{14,10},{16,20},{18,... | collective-permute-start | bytes 221192 | tf_op jit(solution)/shard_map/ppermute | solution.py:466
  52.8 1.7 %collective-permute-start.12 = (bf16[2,144,128]{2,1,0:T(8,128)(2,1)S(1)}, bf16[2,144,128]{2,1,0:T(8,128)(2,1)S(1)}, u32[]{:S(2)}, u32[]{:S(2)}) collective-permute-start(bf16[2,144,128]{2,1,0:T(8,128)(2,1)S(1)} %pad_maximum_fusion.8), channel_id=1, source_target_pairs={{0,8},{2,10},{4,12},{6,14},{8,0},{10,2},{12,4},{14,6},{16,24},{18,... | collective-permute-start | bytes 221192 | tf_op jit(solution)/shard_map/ppermute | solution.py:466
  54.6 0.1 collective-permute-start.13
  54.7 2.8 %collective-permute-start.14 = (bf16[2,144,128]{2,1,0:T(8,128)(2,1)S(1)}, bf16[2,144,128]{2,1,0:T(8,128)(2,1)S(1)}, u32[]{:S(2)}, u32[]{:S(2)}) collective-permute-start(bf16[2,144,128]{2,1,0:T(8,128)(2,1)S(1)} %pad_maximum_fusion.10), channel_id=1, source_target_pairs={{0,16},{2,18},{4,20},{6,22},{8,24},{10,26},{12,28},{14,30},{16,0},... | collective-permute-start | bytes 221192 | tf_op jit(solution)/shard_map/ppermute | solution.py:466
  57.6 1.5 %collective-permute-start.15 = (bf16[2,144,128]{2,1,0:T(8,128)(2,1)S(1)}, bf16[2,144,128]{2,1,0:T(8,128)(2,1)S(1)}, u32[]{:S(2)}, u32[]{:S(2)}) collective-permute-start(bf16[2,144,128]{2,1,0:T(8,128)(2,1)S(1)} %pad_maximum_fusion.11), channel_id=1, source_target_pairs={{0,20},{2,22},{4,16},{6,18},{8,28},{10,30},{12,24},{14,26},{16,4},... | collective-permute-start | bytes 221192 | tf_op jit(solution)/shard_map/ppermute | solution.py:466
  59.1 2.0 %collective-permute-start.16 = (bf16[2,144,128]{2,1,0:T(8,128)(2,1)S(1)}, bf16[2,144,128]{2,1,0:T(8,128)(2,1)S(1)}, u32[]{:S(2)}, u32[]{:S(2)}) collective-permute-start(bf16[2,144,128]{2,1,0:T(8,128)(2,1)S(1)} %pad_maximum_fusion.12), channel_id=1, source_target_pairs={{0,24},{2,26},{4,28},{6,30},{8,16},{10,18},{12,20},{14,22},{16,8},... | collective-permute-start | bytes 221192 | tf_op jit(solution)/shard_map/ppermute | solution.py:466
  61.1 2.3 %collective-permute-start.17 = (bf16[2,144,128]{2,1,0:T(8,128)(2,1)S(1)}, bf16[2,144,128]{2,1,0:T(8,128)(2,1)S(1)}, u32[]{:S(2)}, u32[]{:S(2)}) collective-permute-start(bf16[2,144,128]{2,1,0:T(8,128)(2,1)S(1)} %pad_maximum_fusion.13), channel_id=1, source_target_pairs={{0,28},{2,30},{4,24},{6,26},{8,20},{10,22},{12,16},{14,18},{16,12}... | collective-permute-start | bytes 221192 | tf_op jit(solution)/shard_map/ppermute | solution.py:466
  63.3 1.1 %shard_map.112.refs_0_ = bf16[10,144,128]{2,1,0:T(8,128)(2,1)S(1)} custom-call(s32[16]{0:T(128)S(1)} %copy-done.4, s32[16,10]{1,0:T(8,128)S(1)} %copy-done.3, bf16[8,144,128]{2,1,0:T(8,128)(2,1)S(1)} %get-tuple-element.68.refs_0_, bf16[8,144,128]{2,1,0:T(8,128)(2,1)S(1)} %collective-permute-done.8.refs_1_), custom_call_target="tpu_custom_call" | custom-call | tf_op jit(solution)/shard_map/pallas_call | solution.py:210
  64.4 1.6 %collective-permute-start.18 = (bf16[10,144,128]{2,1,0:T(8,128)(2,1)S(1)}, bf16[10,144,128]{2,1,0:T(8,128)(2,1)S(1)}, u32[]{:S(2)}, u32[]{:S(2)}) collective-permute-start(bf16[10,144,128]{2,1,0:T(8,128)(2,1)S(1)} %shard_map.112.refs_0_), channel_id=1, source_target_pairs={{0,1},{1,0},{2,3},{3,2},{4,5},{5,4},{6,7},{7,6},{8,9},{9,8},{10,11... | collective-permute-start | bytes 1105928 | tf_op jit(solution)/shard_map/ppermute | solution.py:461
  66.0 3.3 %collective-permute-done.15 = bf16[2,144,128]{2,1,0:T(8,128)(2,1)S(1)} collective-permute-done((bf16[2,144,128]{2,1,0:T(8,128)(2,1)S(1)}, bf16[2,144,128]{2,1,0:T(8,128)(2,1)S(1)}, u32[]{:S(2)}, u32[]{:S(2)}) %collective-permute-start.15) | collective-permute-done | bytes 73760 | tf_op jit(solution)/shard_map/ppermute | solution.py:466
  69.4 0.9 shard_map.115.refs_3_
  70.4 1.5 %collective-permute-start.19 = (bf16[10,144,128]{2,1,0:T(8,128)(2,1)S(1)}, bf16[10,144,128]{2,1,0:T(8,128)(2,1)S(1)}, u32[]{:S(2)}, u32[]{:S(2)}) collective-permute-start(bf16[10,144,128]{2,1,0:T(8,128)(2,1)S(1)} %shard_map.115.refs_3_), channel_id=1, source_target_pairs={{0,1},{1,0},{2,3},{3,2},{4,5},{5,4},{6,7},{7,6},{8,9},{9,8},{10,11... | collective-permute-start | bytes 1105928 | tf_op jit(solution)/shard_map/ppermute | solution.py:461
  71.9 0.2 reshape_squeeze.3
  72.2 0.0 copy-start.6
  72.2 0.1 fusion.2
  72.3 0.4 copy.12
  72.7 0.1 copy-done.6
  72.8 3.1 %shard_map.113 = (f32[1024,512]{1,0:T(8,128)S(1)}, f32[1024,128]{1,0:T(8,128)S(1)}, f32[1024,128]{1,0:T(8,128)S(1)}) custom-call(s32[16]{0:T(128)S(1)} %copy-done.4, s32[16]{0:T(128)S(1)} %copy-done.6, bf16[1024,640]{1,0:T(8,128)(2,1)S(1)} %bitcast.27, bf16[10,144,128]{2,1,0:T(8,128)(2,1)S(1)} %shard_map.112.refs_0_), custom_call_target="tpu_custom_call" | custom-call | tf_op jit(solution)/shard_map/pallas_call | solution.py:391
  75.9 0.0 copy-start
  76.0 5.9 %shard_map.116 = (f32[1024,512]{1,0:T(8,128)S(1)}, f32[1024,128]{1,0:T(8,128)S(1)}, f32[1024,128]{1,0:T(8,128)S(1)}) custom-call(s32[16]{0:T(128)S(1)} %copy-done.4, s32[16]{0:T(128)S(1)} %copy-done.6, bf16[1024,640]{1,0:T(8,128)(2,1)S(1)} %bitcast.28, f32[1024,512]{1,0:T(8,128)S(1)} %get-tuple-element.23.refs_0_, ...), custom_call_target="tpu_custom_call" | custom-call | tf_op jit(solution)/shard_map/pallas_call | solution.py:391
  81.9 5.1 %shard_map.117 = (bf16[16,4096]{1,0:T(8,128)(2,1)S(1)}, bf16[16,4096]{1,0:T(8,128)(2,1)S(1)}) custom-call(s32[16]{0:T(128)S(1)} %copy-done.4, s32[16]{0:T(128)S(1)} %copy-done.6, bf16[1024,640]{1,0:T(8,128)(2,1)S(1)} %bitcast.29, bf16[32,512,128]{2,1,0:T(8,128)(2,1)S(1)} %copy-done, f32[1024,512]{1,0:T(8,128)S(1)} %get-tuple-element.30.acc_ref, ...), custom_call_target="tpu_custom_call" | custom-call | tf_op jit(solution)/shard_map/pallas_call | solution.py:414
  87.0 1.4 %collective-permute-start.20 = (bf16[16,4096]{1,0:T(8,128)(2,1)S(1)}, bf16[16,4096]{1,0:T(8,128)(2,1)S(1)}, u32[]{:S(2)}, u32[]{:S(2)}) collective-permute-start(bf16[16,4096]{1,0:T(8,128)(2,1)S(1)} %get-tuple-element.34), channel_id=1, source_target_pairs={{0,1},{1,0},{2,3},{3,2},{4,5},{5,4},{6,7},{7,6},{8,9},{9,8},{10,11... | collective-permute-start | bytes 393224 | tf_op jit(solution)/shard_map/ppermute | solution.py:461
  88.4 3.7 %collective-permute-done.20.refs_1_ = bf16[16,4096]{1,0:T(8,128)(2,1)S(1)} collective-permute-done((bf16[16,4096]{1,0:T(8,128)(2,1)S(1)}, bf16[16,4096]{1,0:T(8,128)(2,1)S(1)}, u32[]{:S(2)}, u32[]{:S(2)}) %collective-permute-start.20) | collective-permute-done | bytes 131104 | tf_op jit(solution)/shard_map/ppermute | solution.py:461
  92.0 0.7 shard_map.118
  (60 shorter events, 0.5 us)
Async XLA Ops:
  6.1 11.1 %collective-permute-start.9 = (f32[4,144,128]{2,1,0:T(8,128)}, f32[4,144,128]{2,1,0:T(8,128)S(1)}, u32[]{:S(2)}, u32[]{:S(2)}) collective-permute-start(f32[4,144,128]{2,1,0:T(8,128)} %get-tuple-element.27), channel_id=1, source_target_pairs={{0,1},{1,0},{2,3},{3,2},{4,5},{5,4},{6,7},{7,6},{8,9},{9,8},{10,11... | collective-permute-start | bytes 884744 | tf_op jit(solution)/shard_map/ppermute | solution.py:461
  9.2 8.1 %copy-start.2 = (f32[4,144,128]{2,1,0:T(8,128)S(1)}, f32[4,144,128]{2,1,0:T(8,128)}, u32[]{:S(2)}) copy-start(f32[4,144,128]{2,1,0:T(8,128)} %get-tuple-element.26.own_ref) | copy-start | bytes 884740
  9.2 8.1 %copy-start.3 = (s32[16,10]{1,0:T(8,128)S(1)}, s32[16,10]{1,0:T(8,128)}, u32[]{:S(2)}) copy-start(s32[16,10]{1,0:T(8,128)} %table_ref.7) | copy-start | bytes 1924
  9.2 8.1 %copy-start.4 = (s32[16]{0:T(128)S(1)}, s32[16]{0:T(128)}, u32[]{:S(2)}) copy-start(s32[16]{0:T(128)} %dest_ref.13) | copy-start | bytes 196
  9.2 8.1 %copy-start.5 = (f32[512]{0:T(512)S(1)}, f32[512]{0:T(512)}, u32[]{:S(2)}) copy-start(f32[512]{0:T(512)} %param.14) | copy-start | bytes 6148
  9.2 8.1 %copy-start.7 = (f32[1,128]{1,0:T(1,128)S(1)}, f32[1,128]{1,0:T(1,128)}, u32[]{:S(2)}) copy-start(f32[1,128]{1,0:T(1,128)} %constant.27.clone.freq_ref) | copy-start | bytes 1540
  9.2 13.5 %copy-start.1 = (f32[4,144,128]{2,1,0:T(8,128)S(1)}, f32[4,144,128]{2,1,0:T(8,128)}, u32[]{:S(2)}) copy-start(f32[4,144,128]{2,1,0:T(8,128)} %get-tuple-element.20.own_ref) | copy-start | bytes 884740
  12.5 10.2 %collective-permute-start = (f32[4,144,128]{2,1,0:T(8,128)}, f32[4,144,128]{2,1,0:T(8,128)S(1)}, u32[]{:S(2)}, u32[]{:S(2)}) collective-permute-start(f32[4,144,128]{2,1,0:T(8,128)} %shard_map.110), channel_id=1, source_target_pairs={{0,1},{1,0},{2,3},{3,2},{4,5},{5,4},{6,7},{7,6},{8,9},{9,8},{10,11... | collective-permute-start | bytes 884744 | tf_op jit(solution)/shard_map/ppermute | solution.py:461
  18.2 32.7 %collective-permute-start.10 = (bf16[8,144,128]{2,1,0:T(8,128)(2,1)S(1)}, bf16[8,144,128]{2,1,0:T(8,128)(2,1)S(1)}, u32[]{:S(2)}, u32[]{:S(2)}) collective-permute-start(bf16[8,144,128]{2,1,0:T(8,128)(2,1)S(1)} %get-tuple-element.29), channel_id=1, source_target_pairs={{0,2},{2,0},{4,6},{6,4},{8,10},{10,8},{12,14},{14,12},{16,18},{18,... | collective-permute-start | bytes 884744 | tf_op jit(solution)/shard_map/ppermute | solution.py:466
  23.7 27.1 %collective-permute-start.7 = (bf16[2,144,128]{2,1,0:T(8,128)(2,1)S(1)}, bf16[2,144,128]{2,1,0:T(8,128)(2,1)S(1)}, u32[]{:S(2)}, u32[]{:S(2)}) collective-permute-start(bf16[2,144,128]{2,1,0:T(8,128)(2,1)S(1)} %pad_maximum_fusion.6), channel_id=1, source_target_pairs={{0,28},{2,30},{4,24},{6,26},{8,20},{10,22},{12,16},{14,18},{16,12}... | collective-permute-start | bytes 221192 | tf_op jit(solution)/shard_map/ppermute | solution.py:466
  28.6 22.2 %collective-permute-start.6 = (bf16[2,144,128]{2,1,0:T(8,128)(2,1)S(1)}, bf16[2,144,128]{2,1,0:T(8,128)(2,1)S(1)}, u32[]{:S(2)}, u32[]{:S(2)}) collective-permute-start(bf16[2,144,128]{2,1,0:T(8,128)(2,1)S(1)} %pad_maximum_fusion.5), channel_id=1, source_target_pairs={{0,24},{2,26},{4,28},{6,30},{8,16},{10,18},{12,20},{14,22},{16,8},... | collective-permute-start | bytes 221192 | tf_op jit(solution)/shard_map/ppermute | solution.py:466
  28.9 21.8 %collective-permute-start.5 = (bf16[2,144,128]{2,1,0:T(8,128)(2,1)S(1)}, bf16[2,144,128]{2,1,0:T(8,128)(2,1)S(1)}, u32[]{:S(2)}, u32[]{:S(2)}) collective-permute-start(bf16[2,144,128]{2,1,0:T(8,128)(2,1)S(1)} %pad_maximum_fusion.4), channel_id=1, source_target_pairs={{0,20},{2,22},{4,16},{6,18},{8,28},{10,30},{12,24},{14,26},{16,4},... | collective-permute-start | bytes 221192 | tf_op jit(solution)/shard_map/ppermute | solution.py:466
  29.7 4.8 %collective-permute-start.1 = (bf16[2,144,128]{2,1,0:T(8,128)(2,1)S(1)}, bf16[2,144,128]{2,1,0:T(8,128)(2,1)S(1)}, u32[]{:S(2)}, u32[]{:S(2)}) collective-permute-start(bf16[2,144,128]{2,1,0:T(8,128)(2,1)S(1)} %pad_maximum_fusion), channel_id=1, source_target_pairs={{0,4},{2,6},{4,0},{6,2},{8,12},{10,14},{12,8},{14,10},{16,20},{18,... | collective-permute-start | bytes 221192 | tf_op jit(solution)/shard_map/ppermute | solution.py:466
  34.5 5.4 %collective-permute-start.2 = (bf16[2,144,128]{2,1,0:T(8,128)(2,1)S(1)}, bf16[2,144,128]{2,1,0:T(8,128)(2,1)S(1)}, u32[]{:S(2)}, u32[]{:S(2)}) collective-permute-start(bf16[2,144,128]{2,1,0:T(8,128)(2,1)S(1)} %pad_maximum_fusion.1), channel_id=1, source_target_pairs={{0,8},{2,10},{4,12},{6,14},{8,0},{10,2},{12,4},{14,6},{16,24},{18,... | collective-permute-start | bytes 221192 | tf_op jit(solution)/shard_map/ppermute | solution.py:466
  39.8 5.6 %collective-permute-start.3 = (bf16[2,144,128]{2,1,0:T(8,128)(2,1)S(1)}, bf16[2,144,128]{2,1,0:T(8,128)(2,1)S(1)}, u32[]{:S(2)}, u32[]{:S(2)}) collective-permute-start(bf16[2,144,128]{2,1,0:T(8,128)(2,1)S(1)} %pad_maximum_fusion.2), channel_id=1, source_target_pairs={{0,12},{2,14},{4,8},{6,10},{8,4},{10,6},{12,0},{14,2},{16,28},{18,... | collective-permute-start | bytes 221192 | tf_op jit(solution)/shard_map/ppermute | solution.py:466
  45.4 5.3 %collective-permute-start.4 = (bf16[2,144,128]{2,1,0:T(8,128)(2,1)S(1)}, bf16[2,144,128]{2,1,0:T(8,128)(2,1)S(1)}, u32[]{:S(2)}, u32[]{:S(2)}) collective-permute-start(bf16[2,144,128]{2,1,0:T(8,128)(2,1)S(1)} %pad_maximum_fusion.3), channel_id=1, source_target_pairs={{0,16},{2,18},{4,20},{6,22},{8,24},{10,26},{12,28},{14,30},{16,0},... | collective-permute-start | bytes 221192 | tf_op jit(solution)/shard_map/ppermute | solution.py:466
  50.8 10.3 %collective-permute-start.8 = (bf16[8,144,128]{2,1,0:T(8,128)(2,1)S(1)}, bf16[8,144,128]{2,1,0:T(8,128)(2,1)S(1)}, u32[]{:S(2)}, u32[]{:S(2)}) collective-permute-start(bf16[8,144,128]{2,1,0:T(8,128)(2,1)S(1)} %get-tuple-element.67), channel_id=1, source_target_pairs={{0,2},{2,0},{4,6},{6,4},{8,10},{10,8},{12,14},{14,12},{16,18},{18,... | collective-permute-start | bytes 884744 | tf_op jit(solution)/shard_map/ppermute | solution.py:466
  50.9 21.0 %copy-start.9 = (bf16[1,32,2048]{2,1,0:T(8,128)(2,1)S(1)}, bf16[1,32,2048]{2,1,0:T(8,128)(2,1)}, u32[]{:S(2)}) copy-start(bf16[1,32,2048]{2,1,0:T(8,128)(2,1)} %param.16) | copy-start | bytes 393220
  50.9 6.6 %collective-permute-start.11 = (bf16[2,144,128]{2,1,0:T(8,128)(2,1)S(1)}, bf16[2,144,128]{2,1,0:T(8,128)(2,1)S(1)}, u32[]{:S(2)}, u32[]{:S(2)}) collective-permute-start(bf16[2,144,128]{2,1,0:T(8,128)(2,1)S(1)} %pad_maximum_fusion.7), channel_id=1, source_target_pairs={{0,4},{2,6},{4,0},{6,2},{8,12},{10,14},{12,8},{14,10},{16,20},{18,... | collective-permute-start | bytes 221192 | tf_op jit(solution)/shard_map/ppermute | solution.py:466
  52.8 6.2 %collective-permute-start.12 = (bf16[2,144,128]{2,1,0:T(8,128)(2,1)S(1)}, bf16[2,144,128]{2,1,0:T(8,128)(2,1)S(1)}, u32[]{:S(2)}, u32[]{:S(2)}) collective-permute-start(bf16[2,144,128]{2,1,0:T(8,128)(2,1)S(1)} %pad_maximum_fusion.8), channel_id=1, source_target_pairs={{0,8},{2,10},{4,12},{6,14},{8,0},{10,2},{12,4},{14,6},{16,24},{18,... | collective-permute-start | bytes 221192 | tf_op jit(solution)/shard_map/ppermute | solution.py:466
  54.6 17.6 %copy-start.8 = (bf16[1,32,32,512]{3,2,1,0:T(8,128)(2,1)S(1)}, bf16[1,32,32,512]{3,2,1,0:T(8,128)(2,1)}, u32[]{:S(2)}) copy-start(bf16[1,32,32,512]{3,2,1,0:T(8,128)(2,1)} %param.15) | copy-start | bytes 3145732
  54.6 9.8 %collective-permute-start.13 = (bf16[2,144,128]{2,1,0:T(8,128)(2,1)S(1)}, bf16[2,144,128]{2,1,0:T(8,128)(2,1)S(1)}, u32[]{:S(2)}, u32[]{:S(2)}) collective-permute-start(bf16[2,144,128]{2,1,0:T(8,128)(2,1)S(1)} %pad_maximum_fusion.9), channel_id=1, source_target_pairs={{0,12},{2,14},{4,8},{6,10},{8,4},{10,6},{12,0},{14,2},{16,28},{18,... | collective-permute-start | bytes 221192 | tf_op jit(solution)/shard_map/ppermute | solution.py:466
  54.7 11.3 %collective-permute-start.14 = (bf16[2,144,128]{2,1,0:T(8,128)(2,1)S(1)}, bf16[2,144,128]{2,1,0:T(8,128)(2,1)S(1)}, u32[]{:S(2)}, u32[]{:S(2)}) collective-permute-start(bf16[2,144,128]{2,1,0:T(8,128)(2,1)S(1)} %pad_maximum_fusion.10), channel_id=1, source_target_pairs={{0,16},{2,18},{4,20},{6,22},{8,24},{10,26},{12,28},{14,30},{16,0},... | collective-permute-start | bytes 221192 | tf_op jit(solution)/shard_map/ppermute | solution.py:466
  57.6 11.8 %collective-permute-start.15 = (bf16[2,144,128]{2,1,0:T(8,128)(2,1)S(1)}, bf16[2,144,128]{2,1,0:T(8,128)(2,1)S(1)}, u32[]{:S(2)}, u32[]{:S(2)}) collective-permute-start(bf16[2,144,128]{2,1,0:T(8,128)(2,1)S(1)} %pad_maximum_fusion.11), channel_id=1, source_target_pairs={{0,20},{2,22},{4,16},{6,18},{8,28},{10,30},{12,24},{14,26},{16,4},... | collective-permute-start | bytes 221192 | tf_op jit(solution)/shard_map/ppermute | solution.py:466
  59.1 10.3 %collective-permute-start.16 = (bf16[2,144,128]{2,1,0:T(8,128)(2,1)S(1)}, bf16[2,144,128]{2,1,0:T(8,128)(2,1)S(1)}, u32[]{:S(2)}, u32[]{:S(2)}) collective-permute-start(bf16[2,144,128]{2,1,0:T(8,128)(2,1)S(1)} %pad_maximum_fusion.12), channel_id=1, source_target_pairs={{0,24},{2,26},{4,28},{6,30},{8,16},{10,18},{12,20},{14,22},{16,8},... | collective-permute-start | bytes 221192 | tf_op jit(solution)/shard_map/ppermute | solution.py:466
  61.1 8.3 %collective-permute-start.17 = (bf16[2,144,128]{2,1,0:T(8,128)(2,1)S(1)}, bf16[2,144,128]{2,1,0:T(8,128)(2,1)S(1)}, u32[]{:S(2)}, u32[]{:S(2)}) collective-permute-start(bf16[2,144,128]{2,1,0:T(8,128)(2,1)S(1)} %pad_maximum_fusion.13), channel_id=1, source_target_pairs={{0,28},{2,30},{4,24},{6,26},{8,20},{10,22},{12,16},{14,18},{16,12}... | collective-permute-start | bytes 221192 | tf_op jit(solution)/shard_map/ppermute | solution.py:466
  64.4 11.5 %collective-permute-start.18 = (bf16[10,144,128]{2,1,0:T(8,128)(2,1)S(1)}, bf16[10,144,128]{2,1,0:T(8,128)(2,1)S(1)}, u32[]{:S(2)}, u32[]{:S(2)}) collective-permute-start(bf16[10,144,128]{2,1,0:T(8,128)(2,1)S(1)} %shard_map.112.refs_0_), channel_id=1, source_target_pairs={{0,1},{1,0},{2,3},{3,2},{4,5},{5,4},{6,7},{7,6},{8,9},{9,8},{10,11... | collective-permute-start | bytes 1105928 | tf_op jit(solution)/shard_map/ppermute | solution.py:461
  70.4 11.5 %collective-permute-start.19 = (bf16[10,144,128]{2,1,0:T(8,128)(2,1)S(1)}, bf16[10,144,128]{2,1,0:T(8,128)(2,1)S(1)}, u32[]{:S(2)}, u32[]{:S(2)}) collective-permute-start(bf16[10,144,128]{2,1,0:T(8,128)(2,1)S(1)} %shard_map.115.refs_3_), channel_id=1, source_target_pairs={{0,1},{1,0},{2,3},{3,2},{4,5},{5,4},{6,7},{7,6},{8,9},{9,8},{10,11... | collective-permute-start | bytes 1105928 | tf_op jit(solution)/shard_map/ppermute | solution.py:461
  72.2 0.7 copy-start.6
  75.9 5.9 %copy-start = (bf16[32,512,128]{2,1,0:T(8,128)(2,1)S(1)}, bf16[32,512,128]{2,1,0:T(8,128)(2,1)}, u32[]{:S(2)}) copy-start(bf16[32,512,128]{2,1,0:T(8,128)(2,1)} %w_ref.1) | copy-start | bytes 12582916
  87.0 5.0 %collective-permute-start.20 = (bf16[16,4096]{1,0:T(8,128)(2,1)S(1)}, bf16[16,4096]{1,0:T(8,128)(2,1)S(1)}, u32[]{:S(2)}, u32[]{:S(2)}) collective-permute-start(bf16[16,4096]{1,0:T(8,128)(2,1)S(1)} %get-tuple-element.34), channel_id=1, source_target_pairs={{0,1},{1,0},{2,3},{3,2},{4,5},{5,4},{6,7},{7,6},{8,9},{9,8},{10,11... | collective-permute-start | bytes 393224 | tf_op jit(solution)/shard_map/ppermute | solution.py:461
